TPU v7x, 128 devices: a whole 4x4x4 slice. The times are simulated.
128 devices in a mesh: gx: 16 (over x, y), gy: 8 (over z, core).
Axes of the slice: x: 4, y: 4, z: 4, core: 2. Of those that a mesh axis runs over, the one named last changes fastest.
Arguments:
- tensor: float32 [256, 512, 1024], P('gx', None, 'gy'), may hold values from -80 to 80
- start_basis: float32 [512, 384], replicated, may hold values from -6 to 6
Outputs:
- core: float32 [256, 384, 1024], P('gx', 'gy')
All inputs are finite; a program needn't handle non-finite values.
Results may differ from a plain program's by a relative error of at most 0.00019.
Values sent between devices are 32-bit elements; how exact they have to be, the bound alone decides.
A program may use at most 512 MiB of HBM per device.

v0:
```python
import jax
import jax.numpy as jnp
from jax import lax
from jax.sharding import PartitionSpec as P

ITERS = 2


def matmul(left, right):
    return jnp.dot(left, right, precision=lax.Precision.HIGHEST, preferred_element_type=jnp.float32)


def orthonormal(product):
    product_gram = matmul(product.T, product)
    lower = jnp.linalg.cholesky(product_gram)
    return jax.scipy.linalg.solve_triangular(lower, product.T, lower=True).T


def body(tensor, start_basis):
    local_gram = lax.dot_general(
        tensor,
        tensor,
        (((0, 2), (0, 2)), ((), ())),
        precision=lax.Precision.HIGHEST,
        preferred_element_type=jnp.float32,
    )
    gram = lax.psum(local_gram, ("gx", "gy"))
    basis = start_basis
    for sweep in range(ITERS):
        product = matmul(gram, basis)
        basis = orthonormal(product)
    core_local = jnp.einsum(
        "ar,kac->krc",
        basis,
        tensor,
        precision=lax.Precision.HIGHEST,
        preferred_element_type=jnp.float32,
    )
    return lax.all_to_all(core_local, "gy", split_axis=1, concat_axis=2, tiled=True)


def solution(mesh):
    placed = (P("gx", None, "gy"), P())
    return jax.shard_map(
        body, mesh=mesh, in_specs=placed, out_specs=P("gx", "gy", None), check_vma=False
    )
```

profile of v0, /device:TPU:1, one launch (start us, length us, event | category | flops | bytes accessed | tf_op | source)
XLA Modules:
  0.0 449.4 jit_solution(3196692239382905080)
XLA Ops:
  6.5 11.5 %convolution_bitcast_fusion.1 = f32[512,512]{1,0:T(8,128)} fusion(f32[16,512,128]{2,1,0:T(8,128)} %param.5), kind=kOutput, calls=%fused_computation.5 | convolution fusion | flops 6442450944 | bytes 5242880 | tf_op jit(solution)/shard_map/dot_general | solution.py:20
  18.1 150.7 %all-reduce.3.cloned.1.call-done = f32[512,512]{1,0:T(8,128)} async-done(((f32[512,512]{1,0:T(8,128)}), f32[512,512]{1,0:T(8,128)}) %all-reduce.3.cloned.1.call-update) | async-done | bytes 1048592 | tf_op jit(solution)/shard_map/psum | solution.py:27
  168.8 3.0 fusion.56
  171.8 1.4 fusion.57
  173.6 0.8 copy-done.2
  174.4 11.7 %cholesky.208 = f32[128,128]{1,0:T(8,128)S(1)} custom-call(f32[128,128]{1,0:T(8,128)S(1)} %cholesky.310), custom_call_target="Cholesky" | custom-call | tf_op jit(solution)/shard_map/jit(cholesky)/cholesky | solution.py:15
  186.1 9.8 %custom-call.20 = f32[1,128,128]{1,2,0:T(8,128)S(1)} custom-call(f32[1,128,128]{2,1,0:T(8,128)S(1)} %get-tuple-element.56), custom_call_target="InvertDiagBlocksLowerTriangular" | custom-call | tf_op jit(solution)/shard_map/jit(cholesky)/cholesky | solution.py:15
  196.0 1.2 constant_dynamic-update-slice_fusion.3
  197.3 1.2 convolution_subtract_fusion.5
  198.5 12.1 %cholesky.227 = f32[128,128]{1,0:T(8,128)S(1)} custom-call(f32[128,128]{1,0:T(8,128)S(1)} %cholesky.314), custom_call_target="Cholesky" | custom-call | tf_op jit(solution)/shard_map/jit(cholesky)/cholesky | solution.py:15
  210.6 9.8 %custom-call.21 = f32[1,128,128]{1,2,0:T(8,128)S(1)} custom-call(f32[1,128,128]{2,1,0:T(8,128)S(1)} %get-tuple-element.53), custom_call_target="InvertDiagBlocksLowerTriangular" | custom-call | tf_op jit(solution)/shard_map/jit(cholesky)/cholesky | solution.py:15
  220.6 1.1 convolution_subtract_fusion.7
  221.8 11.7 %cholesky.246 = f32[128,128]{1,0:T(8,128)S(1)} custom-call(f32[128,128]{1,0:T(8,128)S(1)} %convolution_subtract_fusion.7), custom_call_target="Cholesky" | custom-call | tf_op jit(solution)/shard_map/jit(cholesky)/cholesky | solution.py:15
  233.5 0.7 compare_reduce_fusion.3
  234.2 0.7 compare_reduce_fusion.4
  236.8 0.9 select_select_fusion.1
  237.7 8.7 %while.4 = (s32[]{:T(128)}, f32[384,384]{1,0:T(8,128)}, s32[3,2]{0,1:T(2,128)S(1)}, f32[3,128,128]{2,1,0:T(8,128)S(1)}, s32[]{:T(128)}) while((s32[]{:T(128)}, f32[384,384]{1,0:T(8,128)}, s32[3,2]{0,1:T(2,128)S(1)}, f32[3,128,128]{2,1,0:T(8,128)S(1)}, s32[]{:T(128)}) %tuple.47), condition=%wide.while_cond, body=%wide.while_body.sunk | while | flops 2 | bytes 131189 | solution.py:16
  238.3 2.3 bitcast_dynamic-update-slice_fusion.4
  241.3 2.3 bitcast_dynamic-update-slice_fusion.4
  244.2 2.2 bitcast_dynamic-update-slice_fusion.4
  246.4 29.7 %custom-call.22 = f32[3,128,128]{1,2,0:T(8,128)S(1)} custom-call(f32[3,128,128]{2,1,0:T(8,128)S(1)} %get-tuple-element.21), custom_call_target="InvertDiagBlocksLowerTriangular" | custom-call | tf_op jit(solution)/shard_map/jit(_solve_triangular)/triangular_solve | solution.py:16
  276.5 1.4 convolution_subtract_fusion.3
  278.4 1.9 convolution_subtract_fusion.2
  280.7 1.8 fusion
  282.6 1.4 fusion.58
  284.3 11.7 %cholesky.261 = f32[128,128]{1,0:T(8,128)S(1)} custom-call(f32[128,128]{1,0:T(8,128)S(1)} %cholesky.318), custom_call_target="Cholesky" | custom-call | tf_op jit(solution)/shard_map/jit(cholesky)/cholesky | solution.py:15
  296.1 0.6 compare_reduce_fusion.2
  296.7 10.0 %custom-call.23 = f32[1,128,128]{1,2,0:T(8,128)S(1)} custom-call(f32[1,128,128]{2,1,0:T(8,128)S(1)} %get-tuple-element.49), custom_call_target="InvertDiagBlocksLowerTriangular" | custom-call | tf_op jit(solution)/shard_map/jit(cholesky)/cholesky | solution.py:15
  307.3 11.7 %cholesky.280 = f32[128,128]{1,0:T(8,128)S(1)} custom-call(f32[128,128]{1,0:T(8,128)S(1)} %cholesky.322), custom_call_target="Cholesky" | custom-call | tf_op jit(solution)/shard_map/jit(cholesky)/cholesky | solution.py:15
  319.1 0.7 compare_reduce_fusion.1
  319.8 9.8 %custom-call.24 = f32[1,128,128]{1,2,0:T(8,128)S(1)} custom-call(f32[1,128,128]{2,1,0:T(8,128)S(1)} %get-tuple-element.46), custom_call_target="InvertDiagBlocksLowerTriangular" | custom-call | tf_op jit(solution)/shard_map/jit(cholesky)/cholesky | solution.py:15
  330.1 11.7 %cholesky.299 = f32[128,128]{1,0:T(8,128)S(1)} custom-call(f32[128,128]{1,0:T(8,128)S(1)} %convolution_subtract_fusion.6), custom_call_target="Cholesky" | custom-call | tf_op jit(solution)/shard_map/jit(cholesky)/cholesky | solution.py:15
  341.9 0.6 compare_reduce_fusion
  344.5 6.4 %while.5 = (s32[]{:T(128)}, f32[384,384]{1,0:T(8,128)S(1)}, s32[3,2]{0,1:T(2,128)S(1)}, f32[3,128,128]{2,1,0:T(8,128)S(1)}, s32[]{:T(128)}) while((s32[]{:T(128)}, f32[384,384]{1,0:T(8,128)S(1)}, s32[3,2]{0,1:T(2,128)S(1)}, f32[3,128,128]{2,1,0:T(8,128)S(1)}, s32[]{:T(128)}) %tuple.55), condition=%wide.while_cond.clone, body=%wide.while_body.clone.sunk | while | flops 2 | bytes 131189 | solution.py:16
  344.6 0.6 fusion.80
  345.2 1.4 bitcast_dynamic-update-slice_fusion.5
  346.7 0.6 fusion.80
  347.3 1.4 bitcast_dynamic-update-slice_fusion.5
  348.8 0.6 fusion.80
  349.4 1.4 bitcast_dynamic-update-slice_fusion.5
  350.8 29.7 %custom-call.25 = f32[3,128,128]{1,2,0:T(8,128)S(1)} custom-call(f32[3,128,128]{2,1,0:T(8,128)S(1)} %get-tuple-element.22), custom_call_target="InvertDiagBlocksLowerTriangular" | custom-call | tf_op jit(solution)/shard_map/jit(_solve_triangular)/triangular_solve | solution.py:16
  381.0 0.6 convolution_subtract_fusion.1
  382.0 1.0 convolution_subtract_fusion
  383.5 7.1 %convolution_bitcast_fusion = f32[16,384,128]{2,1,0:T(8,128)S(1)} fusion(f32[16,512,128]{2,1,0:T(8,128)} %param.5, f32[128,512]{1,0:T(8,128)S(1)} %fusion.30, f32[128,512]{1,0:T(8,128)S(1)} %fusion.32, f32[128,512]{1,0:T(8,128)S(1)} %fusion.18), kind=kOutput, calls=%fused_computation.4 | convolution fusion | flops 4832231424 | bytes 8126464 | tf_op jit(solution)/shard_map/ar,kac->krc/dot_general | solution.py:32
  390.6 1.8 copy.8
  392.4 41.7 %all_to_all.18 = f32[16,384,128]{2,0,1:T(8,128)S(1)} all-to-all(f32[16,384,128]{2,0,1:T(8,128)S(1)} %copy.8), channel_id=1, replica_groups=mesh['gx'=16,'gy'=8] {'gy'}, dimensions={1} | all-to-all | bytes 6291456 | tf_op jit(solution)/shard_map/all_to_all | solution.py:39
  434.1 3.5 copy.9
  437.6 4.5 %all_to_all.16 = f32[16,48,1024]{2,1,0:T(8,128)} reshape(f32[16,48,8,128]{3,2,1,0:T(8,128)} %copy.9) | data formatting | bytes 6291456 | tf_op jit(solution)/shard_map/all_to_all | solution.py:39
  (48 shorter events, 6.9 us)
Async XLA Ops:
  6.5 162.3 %copy-start = (f32[512,384]{1,0:T(8,128)S(1)}, f32[512,384]{1,0:T(8,128)}, u32[]{:S(2)}) copy-start(f32[512,384]{1,0:T(8,128)} %param.6) | copy-start | bytes 2359300
  6.5 162.3 %all-reduce.3.cloned.1.call-start = ((), (), s32[]{:S(2)}) async-start(), calls=%async_computation.1 | async-start | bytes 2097152 | tf_op jit(solution)/shard_map/psum | solution.py:27
  173.6 0.8 copy-start.2
  196.0 84.8 %copy-start.1 = (f32[512,512]{1,0:T(8,128)S(1)}, f32[512,512]{1,0:T(8,128)}, u32[]{:S(2)}) copy-start(f32[512,512]{1,0:T(8,128)} %all-reduce.3.cloned.1.call-done) | copy-start | bytes 3145732
Sparse Core Ops, SparseCore 0:
  18.2 150.5 all-reduce.2
where the time goes:
time: 453 us; the launch traced here: 449 us
  other arithmetic  174 us (38%)
  waiting for transfers between devices  151 us (33%)
  blocking collectives  41.7 us (9%)
  matrix products  38.5 us (8%)
  local copies, waits for them, and re-layouts  26.2 us (6%)
  between operations  18 us (4%)
    psum x1, waiting for transfers between devices, body(): gram = lax.psum(local_gram, ('gx', 'gy'))  151 us
    another operation x21, other arithmetic, orthonormal(): lower = jnp.linalg.cholesky(product_gram)  114 us
    another operation x5, other arithmetic, orthonormal(): return jax.scipy.linalg.solve_triangular(lower, product.T, lower=True).T  60.3 us
    all_to_all x1, blocking collectives, body(): lax.all_to_all(core_local, 'gy', split_axis=1, concat_axis=2, tiled=True)  41.7 us
    another operation x21, local copies, waits for them, and re-layouts, orthonormal(): return jax.scipy.linalg.solve_triangular(lower, product.T, lower=True).T  15 us
    dot_general x1, matrix products, body(): lax.dot_general(tensor, tensor, (((0, 2), (0, 2)), ((), ())), precision=l...  11.5 us
  transfers between devices with their start and end apart: 1, of which 1 were waited for; matrix products, arithmetic and copies ran while one was open for 0% of the time, Pallas kernels for 0%

commit v1 on v0

v1 whole, which is shorter than its diff:
```python
import jax
import jax.numpy as jnp
from jax import lax
from jax.experimental import pallas as pl
from jax.experimental.pallas import tpu as pltpu
from jax.sharding import PartitionSpec as P
HI = lax.Precision.HIGHEST
def mm(a, b, ca=1, cb=0):
    return lax.dot_general(a, b, (((ca,), (cb,)), ((), ())), precision=HI, preferred_element_type=jnp.float32)

def rep(x):
    return jnp.broadcast_to(x, (8, 128))

def chol_inv(D):
    A = list(D)
    row = lax.broadcasted_iota(jnp.int32, (8, 128), 0)
    lane = lax.broadcasted_iota(jnp.int32, (8, 128), 1)
    Z = [jnp.where(lane == row + 8 * g, 1.0, 0.0).astype(jnp.float32) for g in range(16)]
    out = []
    for p in range(16):
        c = 8 * p
        S = [[rep(A[p][i:i+1, c+j:c+j+1]) for j in range(i+1)] for i in range(8)]
        V = [rep(A[p][i:i+1, :]) for i in range(8)]
        U = [rep(Z[p][i:i+1, :]) for i in range(8)]
        L = [[None]*8 for _ in range(8)]
        r = [None]*8
        for j in range(8):
            r[j] = lax.rsqrt(S[j][j])
            for i in range(j+1, 8):
                L[i][j] = S[i][j] * r[j]
            for i in range(j+1, 8):
                for k in range(j+1, i+1):
                    S[i][k] = S[i][k] - L[i][j] * L[k][j]
            V[j] = V[j] * r[j]
            U[j] = U[j] * r[j]
            for i in range(j+1, 8):
                V[i] = V[i] - L[i][j] * V[j]
                U[i] = U[i] - L[i][j] * U[j]
        o = U[0]
        for i in range(1, 8):
            o = jnp.where(row == i, U[i], o)
        out.append(o)
        if p == 15:
            break
        F = list(V); FU = list(U)
        for j in range(7, -1, -1):
            F[j] = F[j] * r[j]
            FU[j] = FU[j] * r[j]
            for i in range(j):
                F[i] = F[i] - L[j][i] * F[j]
                FU[i] = FU[i] - L[j][i] * FU[j]
        for g in range(p+1, 16):
            X = [jnp.broadcast_to(A[g][:, c+j:c+j+1], (8, 128)) for j in range(8)]
            def acc(Y, F):
                t = [X[j]*F[j] for j in range(8)]
                t = [t[0]+t[1], t[2]+t[3], t[4]+t[5], t[6]+t[7]]
                return Y - ((t[0]+t[1]) + (t[2]+t[3]))
            Z[g] = acc(Z[g], FU)
            A[g] = acc(A[g], F)
    return out

def qr_kernel(g_ref, b_ref, o_ref, pt, a, li):
    pt[...] = mm(b_ref[...], g_ref[...], 0, 0)
    def it(s, _):
        @pl.when(s == 1)
        def _():
            pt[...] = mm(o_ref[...], g_ref[...])
        a[...] = mm(pt[...], pt[...], 1, 1)
        for kb in range(3):
            k0 = kb*128
            D = [a[k0+8*g:k0+8*g+8, k0:k0+128] for g in range(16)]
            Li = chol_inv(D)
            for g in range(16):
                li[8*g:8*g+8, :] = Li[g]
            Q = mm(li[...], pt[k0:k0+128, :])
            o_ref[k0:k0+128, :] = Q
            if kb < 2:
                R = mm(li[...], a[k0:k0+128, k0+128:])
                a[k0+128:, k0+128:] -= mm(R, R, 0, 0)
                pt[k0+128:, :] -= mm(R, Q, 0, 0)
        return 0
    lax.fori_loop(0, 2, it, 0)

def qr(G, B, **kw):
    return pl.pallas_call(qr_kernel, out_shape=jax.ShapeDtypeStruct((384, 512), jnp.float32),
        in_specs=[pl.BlockSpec(memory_space=pltpu.VMEM)]*2, out_specs=pl.BlockSpec(memory_space=pltpu.VMEM),
        scratch_shapes=[pltpu.VMEM((384,512),jnp.float32), pltpu.VMEM((384,384),jnp.float32), pltpu.VMEM((128,128),jnp.float32)], name="qr", **kw)(G, B)


def body(tensor, start_basis):
    local_gram = lax.dot_general(
        tensor,
        tensor,
        (((0, 2), (0, 2)), ((), ())),
        precision=lax.Precision.HIGHEST,
        preferred_element_type=jnp.float32,
    )
    gram = lax.psum(local_gram, ("gx", "gy"))
    basis_t = qr(gram, start_basis)
    core_local = jnp.einsum(
        "ra,kac->krc",
        basis_t,
        tensor,
        precision=lax.Precision.HIGHEST,
        preferred_element_type=jnp.float32,
    )
    return lax.all_to_all(core_local, "gy", split_axis=1, concat_axis=2, tiled=True)


def solution(mesh):
    placed = (P("gx", None, "gy"), P())
    return jax.shard_map(
        body, mesh=mesh, in_specs=placed, out_specs=P("gx", "gy", None), check_vma=False
    )
```

time: 453 us -> 277 us (0.61)
  other arithmetic: 174 us -> 0 us
  Pallas kernels: 0 us -> 46.6 us
  local copies, waits for them, and re-layouts: 26.2 us -> 5.92 us
  matrix products: 38.5 us -> 18.5 us
  between operations: 18 us -> 13.4 us
    another operation x26 -> x0, other arithmetic: 174 us -> none  [the longest x21 114 us: orthonormal(): lower = jnp.linalg.cholesky(product_gram)]
    pallas_call x0 -> x1, Pallas kernels: none -> 46.6 us  [qr(): pl.pallas_call(qr_kernel, out_shape=jax.ShapeDtypeStruct((384, 512), jnp....]
    another operation x27 -> x0, local copies, waits for them, and re-layouts: 15.1 us -> none  [the longest x21 15 us: orthonormal(): return jax.scipy.linalg.solve_triangular(lower, product.T, lower=True).T]
    another operation x18 -> x0, matrix products: 12.2 us -> none  [the longest x10 7.44 us: orthonormal(): return jax.scipy.linalg.solve_triangular(lower, product.T, lower=True).T]
    dot_general x5 -> x1, matrix products: 14.8 us -> 7.26 us  [body(): jnp.einsum('ra,kac->krc', basis_t, tensor, precision=lax.Precision.HIGHES...]
where the time goes in v1:
time: 277 us
  waiting for transfers between devices  151 us (55%)
  Pallas kernels  46.6 us (17%)
  blocking collectives  41.7 us (15%)
  matrix products  18.5 us (7%)
  between operations  13.4 us (5%)
  local copies, waits for them, and re-layouts  5.92 us (2%)
    psum x1, waiting for transfers between devices, body(): gram = lax.psum(local_gram, ('gx', 'gy'))  151 us
    pallas_call x1, Pallas kernels, qr(): pl.pallas_call(qr_kernel, out_shape=jax.ShapeDtypeStruct((384, 512), jnp....  46.6 us
    all_to_all x1, blocking collectives, body(): lax.all_to_all(core_local, 'gy', split_axis=1, concat_axis=2, tiled=True)  41.7 us
    dot_general x1, matrix products, body(): lax.dot_general(tensor, tensor, (((0, 2), (0, 2)), ((), ())), precision=l...  11.3 us
    dot_general x1, matrix products, body(): jnp.einsum('ra,kac->krc', basis_t, tensor, precision=lax.Precision.HIGHES...  7.26 us
  transfers between devices with their start and end apart: 1, of which 1 were waited for; matrix products, arithmetic and copies ran while one was open for 0% of the time, Pallas kernels for 0%

profile of v1, /device:TPU:1, one launch (start us, length us, event | category | flops | bytes accessed | tf_op | source)
XLA Modules:
  0.0 276.9 jit_solution(5335682071513753832)
XLA Ops:
  6.5 0.0 all-reduce.2.cloned.1.call-start
  6.5 11.3 %convolution_bitcast_fusion.1 = f32[512,512]{1,0:T(8,128)} fusion(f32[16,512,128]{2,1,0:T(8,128)} %param.2), kind=kOutput, calls=%fused_computation.1 | convolution fusion | flops 6442450944 | bytes 5242880 | tf_op jit(solution)/shard_map/dot_general | solution.py:91
  17.8 0.0 all-reduce.2.cloned.1.call-update
  17.8 150.7 %all-reduce.2.cloned.1.call-done.g_ref = f32[512,512]{1,0:T(8,128)} async-done(((f32[512,512]{1,0:T(8,128)}), f32[512,512]{1,0:T(8,128)}) %all-reduce.2.cloned.1.call-update) | async-done | bytes 1048592 | tf_op jit(solution)/shard_map/psum | solution.py:98
  168.6 46.6 %qr.1 = f32[384,512]{1,0:T(8,128)} custom-call(f32[512,512]{1,0:T(8,128)} %all-reduce.2.cloned.1.call-done.g_ref, f32[512,384]{1,0:T(8,128)} %b_ref.1), custom_call_target="tpu_custom_call" | custom-call | tf_op jit(solution)/shard_map/qr/pallas_call | solution.py:85
  215.2 7.3 %convolution_bitcast_fusion = f32[16,384,128]{2,1,0:T(8,128)S(1)} fusion(f32[16,512,128]{2,1,0:T(8,128)} %param.2, f32[384,512]{1,0:T(8,128)} %qr.1), kind=kOutput, calls=%fused_computation | convolution fusion | flops 4831838208 | bytes 8126464 | tf_op jit(solution)/shard_map/ra,kac->krc/dot_general | solution.py:100
  222.5 1.8 copy.4
  224.3 41.7 %all_to_all.18 = f32[16,384,128]{2,0,1:T(8,128)S(1)} all-to-all(f32[16,384,128]{2,0,1:T(8,128)S(1)} %copy.4), channel_id=1, replica_groups=mesh['gx'=16,'gy'=8] {'gy'}, dimensions={1} | all-to-all | bytes 6291456 | tf_op jit(solution)/shard_map/all_to_all | solution.py:107
  266.0 1.8 copy.5
  267.8 2.3 all_to_all.16
Async XLA Ops:
  6.5 162.0 %all-reduce.2.cloned.1.call-start = ((), (), s32[]{:S(2)}) async-start(), calls=%async_computation.1 | async-start | bytes 2097152 | tf_op jit(solution)/shard_map/psum | solution.py:98
Sparse Core Ops, SparseCore 0:
  18.0 150.5 all-reduce.1

commit v2 on v1

--- a/solution.py
+++ b/solution.py
@@ -4,6 +4,125 @@
 from jax.experimental import pallas as pl
 from jax.experimental.pallas import tpu as pltpu
 from jax.sharding import PartitionSpec as P
+MESH = pl.DeviceIdType.MESH
+BF = jnp.bfloat16
+BLOCKS = [(i, j) for i in range(4) for j in range(i + 1)]
+OFFS = sorted(((dx, dy) for dx in range(4) for dy in range(4)), key=lambda o: -(min(o[0], 4 - o[0]) + min(o[1], 4 - o[1])))
+SELF = 15
+NT = (((1,), (1,)), ((), ()))
+
+
+def ar_kernel(t_ref, o_ref, tbuf, hb, lb, gp, ra, aa, rb, ab, rc, ac, tsem, sa, qa, sb, qb, sc, qc, sd, qd, se, qe):
+    gx = lax.axis_index("gx")
+    gy = lax.axis_index("gy")
+    x, y, z, c = gx // 4, gx % 4, gy // 2, gy % 2
+    mate = z * 2 + 1 - c
+
+    def plane(k, sign):
+        dx, dy = OFFS[k]
+        return ((x + sign * dx + 4) % 4) * 4 + (y + sign * dy + 4) % 4
+
+    loads = [pltpu.make_async_copy(t_ref.at[pl.ds(4 * i, 4)], tbuf.at[pl.ds(4 * i, 4)], tsem.at[i]) for i in range(4)]
+    for cp in loads:
+        cp.start()
+    barrier = pltpu.get_barrier_semaphore()
+    pl.semaphore_signal(barrier, inc=1, device_id=(gx, mate), device_id_type=MESH)
+    for k in range(15):
+        pl.semaphore_signal(barrier, inc=1, device_id=(plane(k, 1), gy), device_id_type=MESH)
+    for d in range(1, 4):
+        pl.semaphore_signal(barrier, inc=1, device_id=(gx, ((z + d) % 4) * 2 + c), device_id_type=MESH)
+
+    for i in range(4):
+        loads[i].wait()
+        for s in range(4 * i, 4 * i + 4):
+            v = tbuf[s]
+            h = v.astype(BF)
+            hb[:, 128 * s:128 * s + 128] = h
+            lb[:, 128 * s:128 * s + 128] = (v - h.astype(jnp.float32)).astype(BF)
+
+    def dot(a, b):
+        return lax.dot_general(a, b, NT, preferred_element_type=jnp.float32)
+
+    for (r0, c0) in ((0, 0), (256, 0), (256, 256)):
+        hr, lr = hb[r0:r0 + 256, :], lb[r0:r0 + 256, :]
+        hc, lc = hb[c0:c0 + 256, :], lb[c0:c0 + 256, :]
+        g = dot(hr, hc) + dot(hr, lc) + dot(lr, hc)
+        for n, (i, j) in enumerate(BLOCKS):
+            if r0 <= 128 * i < r0 + 256 and c0 <= 128 * j < c0 + 256:
+                gp[16 * n:16 * n + 16] = g[128 * i - r0:128 * i - r0 + 128, 128 * j - c0:128 * j - c0 + 128].reshape(16, 8, 128)
+
+    pl.semaphore_wait(barrier, 19)
+    pieces = lambda core, g: pl.ds(80 * core + 5 * g, 5)
+
+    def remote(src, dst, ss, rs, dev):
+        return pltpu.make_async_remote_copy(src_ref=src, dst_ref=dst, send_sem=ss, recv_sem=rs, device_id=dev, device_id_type=MESH)
+
+    A = [remote(gp.at[pieces(1 - c, plane(k, 1))], ra.at[k], sa.at[k], qa.at[k], (gx, mate)) for k in range(16)]
+    for cp in A:
+        cp.start()
+    B = []
+    for k in range(16):
+        A[k].wait_recv()
+        aa[k] = gp[pieces(c, plane(k, 1))] + ra[k]
+        if k != SELF:
+            cp = remote(aa.at[k], rb.at[k], sb.at[k], qb.at[k], (plane(k, 1), gy))
+            cp.start()
+            B.append(cp)
+    total = aa[SELF]
+    for k in range(14, -1, -1):
+        B[k].wait_recv()
+        total = total + rb[k]
+    ab[...] = total
+    rc[z] = total
+    C = []
+    for d in range(1, 4):
+        cp = remote(ab, rc.at[z], sc.at[d], qc.at[d], (gx, ((z + d) % 4) * 2 + c))
+        cp.start()
+        C.append(cp)
+    for cp in C:
+        cp.wait_recv()
+    total = (rc[0] + rc[1]) + (rc[2] + rc[3])
+    ac[...] = total
+    mine = pieces(c, gx)
+    D = []
+    for k in range(15):
+        cp = remote(ac, o_ref.at[mine], sd.at[k], qd.at[k], (plane(k, 1), gy))
+        cp.start()
+        D.append(cp)
+    o_ref[mine] = total
+    E = [remote(ac, o_ref.at[mine], se.at[SELF], qe.at[SELF], (gx, mate))]
+    E[0].start()
+    for k in range(14, -1, -1):
+        D[k].wait_recv()
+        spot = pieces(c, plane(k, -1))
+        cp = remote(o_ref.at[spot], o_ref.at[spot], se.at[k], qe.at[k], (gx, mate))
+        cp.start()
+        E.append(cp)
+    for cp in E:
+        cp.wait_recv()
+    for cp in A + B + C + D + E:
+        cp.wait_send()
+
+
+def gram_sum(tensor):
+    f = jnp.float32
+    V, D = pltpu.VMEM, pltpu.SemaphoreType.DMA
+    return pl.pallas_call(
+        ar_kernel,
+        out_shape=jax.ShapeDtypeStruct((160, 8, 128), f),
+        in_specs=[pl.BlockSpec(memory_space=pl.ANY)],
+        out_specs=pl.BlockSpec(memory_space=pltpu.VMEM),
+        scratch_shapes=[
+            V((16, 512, 128), f), V((512, 2048), BF), V((512, 2048), BF),
+            V((160, 8, 128), f), V((16, 5, 8, 128), f), V((16, 5, 8, 128), f), V((16, 5, 8, 128), f),
+            V((5, 8, 128), f), V((4, 5, 8, 128), f), V((5, 8, 128), f),
+            D((4,)), D((16,)), D((16,)), D((16,)), D((16,)), D((4,)), D((4,)), D((16,)), D((16,)), D((16,)), D((16,)),
+        ],
+        compiler_params=pltpu.CompilerParams(collective_id=0, has_side_effects=True, vmem_limit_bytes=40 << 20),
+        name="gram_sum",
+    )(tensor)
+
+
 HI = lax.Precision.HIGHEST
 def mm(a, b, ca=1, cb=0):
     return lax.dot_general(a, b, (((ca,), (cb,)), ((), ())), precision=HI, preferred_element_type=jnp.float32)
@@ -59,7 +178,15 @@
             A[g] = acc(A[g], F)
     return out
 
-def qr_kernel(g_ref, b_ref, o_ref, pt, a, li):
+def qr_kernel(p_ref, b_ref, o_ref, g_ref, pt, a, li):
+    n = 0
+    for i in range(4):
+        for j in range(i + 1):
+            blk = p_ref[16*n:16*n+16].reshape(128, 128)
+            g_ref[128*i:128*i+128, 128*j:128*j+128] = blk
+            if j < i:
+                g_ref[128*j:128*j+128, 128*i:128*i+128] = blk.T
+            n += 1
     pt[...] = mm(b_ref[...], g_ref[...], 0, 0)
     def it(s, _):
         @pl.when(s == 1)
@@ -84,19 +211,11 @@
 def qr(G, B, **kw):
     return pl.pallas_call(qr_kernel, out_shape=jax.ShapeDtypeStruct((384, 512), jnp.float32),
         in_specs=[pl.BlockSpec(memory_space=pltpu.VMEM)]*2, out_specs=pl.BlockSpec(memory_space=pltpu.VMEM),
-        scratch_shapes=[pltpu.VMEM((384,512),jnp.float32), pltpu.VMEM((384,384),jnp.float32), pltpu.VMEM((128,128),jnp.float32)], name="qr", **kw)(G, B)
+        scratch_shapes=[pltpu.VMEM((512,512),jnp.float32), pltpu.VMEM((384,512),jnp.float32), pltpu.VMEM((384,384),jnp.float32), pltpu.VMEM((128,128),jnp.float32)], name="qr", **kw)(G, B)
 
 
 def body(tensor, start_basis):
-    local_gram = lax.dot_general(
-        tensor,
-        tensor,
-        (((0, 2), (0, 2)), ((), ())),
-        precision=lax.Precision.HIGHEST,
-        preferred_element_type=jnp.float32,
-    )
-    gram = lax.psum(local_gram, ("gx", "gy"))
-    basis_t = qr(gram, start_basis)
+    basis_t = qr(gram_sum(tensor), start_basis)
     core_local = jnp.einsum(
         "ra,kac->krc",
         basis_t,

time: 277 us -> 133 us (0.48)
  waiting for transfers between devices: 151 us -> 0 us
  Pallas kernels: 46.6 us -> 76.2 us
  between operations: 13.4 us -> 0.04 us
  matrix products: 18.5 us -> 7.26 us
  local copies, waits for them, and re-layouts: 5.92 us -> 8.94 us
    psum x1 -> x0, waiting for transfers between devices: 151 us -> none  [body(): gram = lax.psum(local_gram, ('gx', 'gy'))]
    pallas_call x0 -> x1, Pallas kernels: none -> 29.6 us  [gram_sum(): pl.pallas_call(ar_kernel, out_shape=jax.ShapeDtypeStruct((160, 8, 128), f...]
    dot_general x1 -> x0, matrix products: 11.3 us -> none  [body(): lax.dot_general(tensor, tensor, (((0, 2), (0, 2)), ((), ())), precision=l...]
    unnamed x0 -> x4, local copies, waits for them, and re-layouts: none -> 3.02 us
  transfers between devices with their start and end apart: 1 -> 0, of which waited for: 1 -> 0; matrix products, arithmetic and copies ran while one was open for 0% -> 0% of each run, Pallas kernels for 0% -> 0%
where the time goes in v2:
time: 133 us
  Pallas kernels  76.2 us (57%)
  blocking collectives  40.4 us (30%)
  local copies, waits for them, and re-layouts  8.94 us (7%)
  matrix products  7.26 us (5%)
    pallas_call x1, Pallas kernels, qr(): pl.pallas_call(qr_kernel, out_shape=jax.ShapeDtypeStruct((384, 512), jnp....  46.6 us
    all_to_all x1, blocking collectives, body(): lax.all_to_all(core_local, 'gy', split_axis=1, concat_axis=2, tiled=True)  40.4 us
    pallas_call x1, Pallas kernels, gram_sum(): pl.pallas_call(ar_kernel, out_shape=jax.ShapeDtypeStruct((160, 8, 128), f...  29.6 us
    dot_general x1, matrix products, body(): jnp.einsum('ra,kac->krc', basis_t, tensor, precision=lax.Precision.HIGHES...  7.26 us
    all_to_all x2, local copies, waits for them, and re-layouts, body(): lax.all_to_all(core_local, 'gy', split_axis=1, concat_axis=2, tiled=True)  4.1 us
    unnamed x4, local copies, waits for them, and re-layouts  3.02 us

profile of v2, /device:TPU:1, one launch (start us, length us, event | category | flops | bytes accessed | tf_op | source)
XLA Modules:
  0.0 132.9 jit_solution(5964078321774078479)
XLA Ops:
  0.0 0.0 copy-start
  0.0 2.2 %copy-done = f32[16,512,128]{2,1,0:T(8,128)S(1)} copy-done((f32[16,512,128]{2,1,0:T(8,128)S(1)}, f32[16,512,128]{2,1,0:T(8,128)}, u32[]{:S(2)}) %copy-start) | copy-done | bytes 4194328
  2.2 29.6 %gram_sum.1.p_ref = f32[160,8,128]{2,1,0:T(8,128)S(1)} custom-call(f32[16,512,128]{2,1,0:T(8,128)S(1)} %copy-done), custom_call_target="tpu_custom_call" | custom-call | tf_op jit(solution)/shard_map/gram_sum/pallas_call | solution.py:110
  31.8 0.0 copy-start.1
  31.8 0.8 copy-done.1
  32.6 46.6 %qr.1 = f32[384,512]{1,0:T(8,128)} custom-call(f32[160,8,128]{2,1,0:T(8,128)} %copy-done.1, f32[512,384]{1,0:T(8,128)} %b_ref.1), custom_call_target="tpu_custom_call" | custom-call | tf_op jit(solution)/shard_map/qr/pallas_call | solution.py:212
  79.3 7.3 %convolution_bitcast_fusion = f32[16,384,128]{2,1,0:T(8,128)S(1)} fusion(f32[16,512,128]{2,1,0:T(8,128)} %t_ref.1, f32[384,512]{1,0:T(8,128)} %qr.1), kind=kOutput, calls=%fused_computation | convolution fusion | flops 4831838208 | bytes 8126464 | tf_op jit(solution)/shard_map/ra,kac->krc/dot_general | solution.py:219
  86.5 1.8 %copy.4 = f32[16,384,128]{2,0,1:T(8,128)S(1)} copy(f32[16,384,128]{2,1,0:T(8,128)S(1)} %convolution_bitcast_fusion) | data formatting | bytes 6291456 | tf_op jit(solution)/shard_map/ra,kac->krc/transpose | solution.py:219
  88.4 40.4 %all_to_all.18 = f32[16,384,128]{2,0,1:T(8,128)S(1)} all-to-all(f32[16,384,128]{2,0,1:T(8,128)S(1)} %copy.4), channel_id=1, replica_groups=mesh['gx'=16,'gy'=8] {'gy'}, dimensions={1} | all-to-all | bytes 6291456 | tf_op jit(solution)/shard_map/all_to_all | solution.py:226
  128.8 1.8 %copy.5 = f32[16,48,8,128]{3,2,1,0:T(8,128)S(1)} copy(f32[16,48,8,128]{3,0,1,2:T(8,128)S(1)} %bitcast.11) | data formatting | bytes 6291456 | tf_op jit(solution)/shard_map/all_to_all | solution.py:226
  130.6 2.3 %all_to_all.16 = f32[16,48,1024]{2,1,0:T(8,128)} reshape(f32[16,48,8,128]{3,2,1,0:T(8,128)S(1)} %copy.5) | data formatting | bytes 6291456 | tf_op jit(solution)/shard_map/all_to_all | solution.py:226
Async XLA Ops:
  0.0 2.2 %copy-start = (f32[16,512,128]{2,1,0:T(8,128)S(1)}, f32[16,512,128]{2,1,0:T(8,128)}, u32[]{:S(2)}) copy-start(f32[16,512,128]{2,1,0:T(8,128)} %t_ref.1) | copy-start | bytes 12582916
  31.8 0.8 copy-start.1

commit v3 on v2

--- a/solution.py
+++ b/solution.py
@@ -118,7 +118,7 @@
             V((5, 8, 128), f), V((4, 5, 8, 128), f), V((5, 8, 128), f),
             D((4,)), D((16,)), D((16,)), D((16,)), D((16,)), D((4,)), D((4,)), D((16,)), D((16,)), D((16,)), D((16,)),
         ],
-        compiler_params=pltpu.CompilerParams(collective_id=0, has_side_effects=True, vmem_limit_bytes=40 << 20),
+        compiler_params=pltpu.CompilerParams(collective_id=0, has_side_effects=True, vmem_limit_bytes=62 << 20),
         name="gram_sum",
     )(tensor)
 
@@ -214,16 +214,80 @@
         scratch_shapes=[pltpu.VMEM((512,512),jnp.float32), pltpu.VMEM((384,512),jnp.float32), pltpu.VMEM((384,384),jnp.float32), pltpu.VMEM((128,128),jnp.float32)], name="qr", **kw)(G, B)
 
 
+RELS = [(2, 0), (2, 1), (1, 0), (3, 0), (1, 1), (3, 1), (0, 1)]
+GROUPS = [(0, 2), (2, 4), (4, 8), (8, 12), (12, 16)]
+
+
+def core_kernel(q_ref, t_ref, o_ref, tbuf, qh, ql, y, tsem, ssem, rsem, osem):
+    gx = lax.axis_index("gx")
+    gy = lax.axis_index("gy")
+    z, c = gy // 2, gy % 2
+
+    def other(r):
+        dz, dc = RELS[r]
+        return ((z + dz) % 4) * 2 + (c + dc) % 2
+
+    loads = [pltpu.make_async_copy(t_ref.at[pl.ds(a, b - a)], tbuf.at[pl.ds(a, b - a)], tsem.at[n]) for n, (a, b) in enumerate(GROUPS)]
+    for cp in loads:
+        cp.start()
+    barrier = pltpu.get_barrier_semaphore()
+    for r in range(7):
+        pl.semaphore_signal(barrier, inc=1, device_id=(gx, other(r)), device_id_type=pl.DeviceIdType.MESH)
+    v = q_ref[...]
+    h = v.astype(jnp.bfloat16)
+    qh[...] = h
+    ql[...] = (v - h.astype(jnp.float32)).astype(jnp.bfloat16)
+
+    def dot(a, b):
+        return jnp.dot(a, b, preferred_element_type=jnp.float32)
+
+    spot = pl.ds(pl.multiple_of(gy * 128, 128), 128)
+    sends = []
+    for n, (a, b) in enumerate(GROUPS):
+        loads[n].wait()
+        for k in range(a, b, 2):
+            v = jnp.concatenate([tbuf[k], tbuf[k + 1]], axis=1)
+            th = v.astype(jnp.bfloat16)
+            tl = (v - th.astype(jnp.float32)).astype(jnp.bfloat16)
+            out = dot(qh[...], th) + dot(qh[...], tl) + dot(ql[...], th)
+            y[k] = out[:, :128]
+            y[k + 1] = out[:, 128:]
+        if n == 0:
+            pl.semaphore_wait(barrier, 7)
+        for r in range(7):
+            cp = pltpu.make_async_remote_copy(
+                src_ref=y.at[pl.ds(a, b - a), pl.ds(pl.multiple_of(48 * other(r), 8), 48)],
+                dst_ref=o_ref.at[pl.ds(a, b - a), pl.ds(0, 48), spot],
+                send_sem=ssem.at[r, n], recv_sem=rsem.at[r, n],
+                device_id=(gx, other(r)), device_id_type=pl.DeviceIdType.MESH)
+            cp.start()
+            sends.append(cp)
+    own = pltpu.make_async_copy(y.at[pl.ds(0, 16), pl.ds(pl.multiple_of(48 * gy, 8), 48)], o_ref.at[pl.ds(0, 16), pl.ds(0, 48), spot], osem)
+    own.start()
+    for cp in sends:
+        cp.wait()
+    own.wait()
+
+
+def core_out(basis_t, tensor):
+    f = jnp.float32
+    V, D = pltpu.VMEM, pltpu.SemaphoreType.DMA
+    ng = len(GROUPS)
+    return pl.pallas_call(
+        core_kernel,
+        out_shape=jax.ShapeDtypeStruct((16, 48, 1024), f),
+        in_specs=[pl.BlockSpec(memory_space=pltpu.VMEM), pl.BlockSpec(memory_space=pl.ANY)],
+        out_specs=pl.BlockSpec(memory_space=pl.ANY),
+        scratch_shapes=[V((16, 512, 128), f), V((384, 512), jnp.bfloat16), V((384, 512), jnp.bfloat16), V((16, 384, 128), f),
+                        D((ng,)), D((7, ng)), D((7, ng)), D],
+        compiler_params=pltpu.CompilerParams(collective_id=1, has_side_effects=True, vmem_limit_bytes=62 << 20),
+        name="core_out",
+    )(basis_t, tensor)
+
+
 def body(tensor, start_basis):
     basis_t = qr(gram_sum(tensor), start_basis)
-    core_local = jnp.einsum(
-        "ra,kac->krc",
-        basis_t,
-        tensor,
-        precision=lax.Precision.HIGHEST,
-        preferred_element_type=jnp.float32,
-    )
-    return lax.all_to_all(core_local, "gy", split_axis=1, concat_axis=2, tiled=True)
+    return core_out(basis_t, tensor)
 
 
 def solution(mesh):

time: 133 us -> 121 us (0.910)
  Pallas kernels: 76.2 us -> 117 us
  blocking collectives: 40.4 us -> 0 us
  matrix products: 7.26 us -> 0 us
  local copies, waits for them, and re-layouts: 8.94 us -> 3.97 us
    all_to_all x1 -> x0, blocking collectives: 40.4 us -> none  [body(): lax.all_to_all(core_local, 'gy', split_axis=1, concat_axis=2, tiled=True)]
    pallas_call x0 -> x1, Pallas kernels: none -> 39.3 us  [core_out(): pl.pallas_call(core_kernel, out_shape=jax.ShapeDtypeStruct((16, 48, 1024)...]
    dot_general x1 -> x0, matrix products: 7.26 us -> none  [body(): jnp.einsum('ra,kac->krc', basis_t, tensor, precision=lax.Precision.HIGHES...]
    all_to_all x2 -> x0, local copies, waits for them, and re-layouts: 4.1 us -> none  [body(): lax.all_to_all(core_local, 'gy', split_axis=1, concat_axis=2, tiled=True)]
    transpose x1 -> x0, local copies, waits for them, and re-layouts: 1.82 us -> none  [body(): jnp.einsum('ra,kac->krc', basis_t, tensor, precision=lax.Precision.HIGHES...]
    pallas_call x1, Pallas kernels: 29.6 us -> 31 us  [gram_sum(): pl.pallas_call(ar_kernel, out_shape=jax.ShapeDtypeStruct((160, 8, 128), f...]
    unnamed x4 -> x1, local copies, waits for them, and re-layouts: 3.02 us -> 3.97 us
where the time goes in v3:
time: 121 us
  Pallas kernels  117 us (97%)
  local copies, waits for them, and re-layouts  3.97 us (3%)
    pallas_call x1, Pallas kernels, qr(): pl.pallas_call(qr_kernel, out_shape=jax.ShapeDtypeStruct((384, 512), jnp....  46.6 us
    pallas_call x1, Pallas kernels, core_out(): pl.pallas_call(core_kernel, out_shape=jax.ShapeDtypeStruct((16, 48, 1024)...  39.3 us
    pallas_call x1, Pallas kernels, gram_sum(): pl.pallas_call(ar_kernel, out_shape=jax.ShapeDtypeStruct((160, 8, 128), f...  31 us
    unnamed x1, local copies, waits for them, and re-layouts  3.97 us

profile of v3, /device:TPU:1, one launch (start us, length us, event | category | flops | bytes accessed | tf_op | source)
XLA Modules:
  0.0 120.9 jit_solution(1361571538411350327)
XLA Ops:
  0.0 31.0 %gram_sum.1.p_ref = f32[160,8,128]{2,1,0:T(8,128)} custom-call(f32[16,512,128]{2,1,0:T(8,128)} %t_ref.3), custom_call_target="tpu_custom_call" | custom-call | tf_op jit(solution)/shard_map/gram_sum/pallas_call | solution.py:110
  31.0 46.6 %qr.1.q_ref = f32[384,512]{1,0:T(8,128)} custom-call(f32[160,8,128]{2,1,0:T(8,128)} %gram_sum.1.p_ref, f32[512,384]{1,0:T(8,128)} %b_ref.1), custom_call_target="tpu_custom_call" | custom-call | tf_op jit(solution)/shard_map/qr/pallas_call | solution.py:212
  77.7 39.3 %core_out.1 = f32[16,48,1024]{2,1,0:T(8,128)} custom-call(f32[384,512]{1,0:T(8,128)} %qr.1.q_ref, f32[16,512,128]{2,1,0:T(8,128)} %t_ref.3), custom_call_target="tpu_custom_call" | custom-call | tf_op jit(solution)/shard_map/core_out/pallas_call | solution.py:276
  117.0 4.0 %copy.4 = f32[16,48,1024]{2,1,0:T(8,128)} copy(f32[16,48,1024]{2,1,0:T(8,128)} %core_out.1) | data formatting | bytes 6291456

commit v4 on v3

--- a/solution.py
+++ b/solution.py
@@ -178,47 +178,74 @@
             A[g] = acc(A[g], F)
     return out
 
-def qr_kernel(p_ref, b_ref, o_ref, g_ref, pt, a, li):
+def sweep(pt, a, o_ref, li):
+    a[...] = mm(pt[...], pt[...], 1, 1)
+
+    def block(kb, _):
+        k0 = pl.multiple_of(kb * 128, 128)
+        Li = chol_inv([a[pl.ds(k0 + 8 * g, 8), pl.ds(k0, 128)] for g in range(16)])
+        for g in range(16):
+            li[8 * g:8 * g + 8, :] = Li[g]
+        for n in range(3):
+            @pl.when(kb == n)
+            def _():
+                lo, hi = 128 * n, 128 * n + 128
+                Q = mm(li[...], pt[lo:hi, :])
+                o_ref[lo:hi, :] = Q
+                if n < 2:
+                    R = mm(li[...], a[lo:hi, hi:])
+                    a[hi:, hi:] -= mm(R, R, 0, 0)
+                    pt[hi:, :] -= mm(R, Q, 0, 0)
+        return 0
+
+    lax.fori_loop(0, 3, block, 0)
+
+
+def first_kernel(p_ref, b_ref, g_ref, o_ref, pt, a, li):
     n = 0
     for i in range(4):
         for j in range(i + 1):
-            blk = p_ref[16*n:16*n+16].reshape(128, 128)
-            g_ref[128*i:128*i+128, 128*j:128*j+128] = blk
+            blk = p_ref[16 * n:16 * n + 16].reshape(128, 128)
+            g_ref[128 * i:128 * i + 128, 128 * j:128 * j + 128] = blk
             if j < i:
-                g_ref[128*j:128*j+128, 128*i:128*i+128] = blk.T
+                g_ref[128 * j:128 * j + 128, 128 * i:128 * i + 128] = blk.T
             n += 1
     pt[...] = mm(b_ref[...], g_ref[...], 0, 0)
-    def it(s, _):
-        @pl.when(s == 1)
-        def _():
-            pt[...] = mm(o_ref[...], g_ref[...])
-        a[...] = mm(pt[...], pt[...], 1, 1)
-        for kb in range(3):
-            k0 = kb*128
-            D = [a[k0+8*g:k0+8*g+8, k0:k0+128] for g in range(16)]
-            Li = chol_inv(D)
-            for g in range(16):
-                li[8*g:8*g+8, :] = Li[g]
-            Q = mm(li[...], pt[k0:k0+128, :])
-            o_ref[k0:k0+128, :] = Q
-            if kb < 2:
-                R = mm(li[...], a[k0:k0+128, k0+128:])
-                a[k0+128:, k0+128:] -= mm(R, R, 0, 0)
-                pt[k0+128:, :] -= mm(R, Q, 0, 0)
-        return 0
-    lax.fori_loop(0, 2, it, 0)
-
-def qr(G, B, **kw):
-    return pl.pallas_call(qr_kernel, out_shape=jax.ShapeDtypeStruct((384, 512), jnp.float32),
-        in_specs=[pl.BlockSpec(memory_space=pltpu.VMEM)]*2, out_specs=pl.BlockSpec(memory_space=pltpu.VMEM),
-        scratch_shapes=[pltpu.VMEM((512,512),jnp.float32), pltpu.VMEM((384,512),jnp.float32), pltpu.VMEM((384,384),jnp.float32), pltpu.VMEM((128,128),jnp.float32)], name="qr", **kw)(G, B)
+    sweep(pt, a, o_ref, li)
+
+
+def second_kernel(g_ref, q_ref, o_ref, pt, a, li):
+    pt[...] = mm(q_ref[...], g_ref[...])
+    sweep(pt, a, o_ref, li)
+
+
+SCRATCH = [pltpu.VMEM((384, 512), jnp.float32), pltpu.VMEM((384, 384), jnp.float32), pltpu.VMEM((128, 128), jnp.float32)]
+WHOLE = pl.BlockSpec(memory_space=pltpu.VMEM)
+COST = pl.CostEstimate(flops=2000000000, bytes_accessed=3000000, transcendentals=0)
+
+
+def sweep_first(packed, start):
+    return pl.pallas_call(
+        first_kernel,
+        out_shape=(jax.ShapeDtypeStruct((512, 512), jnp.float32), jax.ShapeDtypeStruct((384, 512), jnp.float32)),
+        in_specs=[WHOLE] * 2, out_specs=(WHOLE, WHOLE), scratch_shapes=SCRATCH, cost_estimate=COST, name="sweep_first",
+    )(packed, start)
+
+
+def sweep_second(gram, basis_t):
+    return pl.pallas_call(
+        second_kernel,
+        out_shape=jax.ShapeDtypeStruct((384, 512), jnp.float32),
+        in_specs=[WHOLE] * 2, out_specs=WHOLE, scratch_shapes=SCRATCH, cost_estimate=COST, name="sweep_second",
+    )(gram, basis_t)
 
 
 RELS = [(2, 0), (2, 1), (1, 0), (3, 0), (1, 1), (3, 1), (0, 1)]
-GROUPS = [(0, 2), (2, 4), (4, 8), (8, 12), (12, 16)]
-
-
-def core_kernel(q_ref, t_ref, o_ref, tbuf, qh, ql, y, tsem, ssem, rsem, osem):
+KG = 8
+GROUPS = [(0, 2), (2, 4), (4, 8)]
+
+
+def core_kernel(q_ref, t_ref, g1a, g1b, g3a, g3b, g2a, g2b, o_ref, tbuf, gbuf, qh, ql, y, yg, tsem, gsem, ssem, rsem, xsem, wsem, osem):
     gx = lax.axis_index("gx")
     gy = lax.axis_index("gy")
     z, c = gy // 2, gy % 2
@@ -227,9 +254,16 @@
         dz, dc = RELS[r]
         return ((z + dz) % 4) * 2 + (c + dc) % 2
 
-    loads = [pltpu.make_async_copy(t_ref.at[pl.ds(a, b - a)], tbuf.at[pl.ds(a, b - a)], tsem.at[n]) for n, (a, b) in enumerate(GROUPS)]
+    na = 16 - KG
+    loads = [pltpu.make_async_copy(t_ref.at[pl.ds(KG + a, b - a)], tbuf.at[pl.ds(a, b - a)], tsem.at[n]) for n, (a, b) in enumerate(GROUPS)]
+    half = KG // 2
+    gloads = [[pltpu.make_async_copy(t_ref.at[pl.ds(half * n, half)] if r is None else r, gbuf.at[s, pl.ds(half * n, half)], gsem.at[s, n]) for n, r in enumerate(p)]
+              for s, p in enumerate(((None, None), (g1a, g1b), (g3a, g3b), (g2a, g2b)))]
     for cp in loads:
         cp.start()
+    for cps in gloads:
+        for cp in cps:
+            cp.start()
     barrier = pltpu.get_barrier_semaphore()
     for r in range(7):
         pl.semaphore_signal(barrier, inc=1, device_id=(gx, other(r)), device_id_type=pl.DeviceIdType.MESH)
@@ -241,14 +275,18 @@
     def dot(a, b):
         return jnp.dot(a, b, preferred_element_type=jnp.float32)
 
-    spot = pl.ds(pl.multiple_of(gy * 128, 128), 128)
+    def split(v):
+        th = v.astype(jnp.bfloat16)
+        return th, (v - th.astype(jnp.float32)).astype(jnp.bfloat16)
+
+    def cols(dev):
+        return pl.ds(pl.multiple_of(dev * 128, 128), 128)
+
     sends = []
     for n, (a, b) in enumerate(GROUPS):
         loads[n].wait()
         for k in range(a, b, 2):
-            v = jnp.concatenate([tbuf[k], tbuf[k + 1]], axis=1)
-            th = v.astype(jnp.bfloat16)
-            tl = (v - th.astype(jnp.float32)).astype(jnp.bfloat16)
+            th, tl = split(jnp.concatenate([tbuf[k], tbuf[k + 1]], axis=1))
             out = dot(qh[...], th) + dot(qh[...], tl) + dot(ql[...], th)
             y[k] = out[:, :128]
             y[k + 1] = out[:, 128:]
@@ -257,37 +295,76 @@
         for r in range(7):
             cp = pltpu.make_async_remote_copy(
                 src_ref=y.at[pl.ds(a, b - a), pl.ds(pl.multiple_of(48 * other(r), 8), 48)],
-                dst_ref=o_ref.at[pl.ds(a, b - a), pl.ds(0, 48), spot],
+                dst_ref=o_ref.at[pl.ds(KG + a, b - a), pl.ds(0, 48), cols(gy)],
                 send_sem=ssem.at[r, n], recv_sem=rsem.at[r, n],
                 device_id=(gx, other(r)), device_id_type=pl.DeviceIdType.MESH)
             cp.start()
             sends.append(cp)
-    own = pltpu.make_async_copy(y.at[pl.ds(0, 16), pl.ds(pl.multiple_of(48 * gy, 8), 48)], o_ref.at[pl.ds(0, 16), pl.ds(0, 48), spot], osem)
+    own = pltpu.make_async_copy(y.at[pl.ds(0, na), pl.ds(pl.multiple_of(48 * gy, 8), 48)], o_ref.at[pl.ds(KG, na), pl.ds(0, 48), cols(gy)], osem.at[4])
     own.start()
+    rows = pl.ds(pl.multiple_of(96 * z, 32), 96)
+    q2 = jnp.concatenate([qh[rows, :], ql[rows, :]], axis=0)
+    locs = [own]
+    for s, dz in enumerate((0, 3, 1, 2)):
+        for cp in gloads[s]:
+            cp.wait()
+        for k in range(0, KG, 2):
+            th, tl = split(jnp.concatenate([gbuf[s, k], gbuf[s, k + 1]], axis=1))
+            o2 = dot(q2, th)
+            out = o2[:96] + o2[96:] + dot(q2[:96], tl)
+            for d in range(2):
+                yg[s, 0, k + d] = out[:48, 128 * d:128 * d + 128]
+                yg[s, 1, k + d] = out[48:, 128 * d:128 * d + 128]
+        src = ((z + dz) % 4) * 2 + c
+        cp = pltpu.make_async_remote_copy(
+            src_ref=yg.at[s, 1 - c], dst_ref=o_ref.at[pl.ds(0, KG), pl.ds(0, 48), cols(src)],
+            send_sem=xsem.at[s], recv_sem=wsem.at[s],
+            device_id=(gx, z * 2 + 1 - c), device_id_type=pl.DeviceIdType.MESH)
+        cp.start()
+        sends.append(cp)
+        cp = pltpu.make_async_copy(yg.at[s, c], o_ref.at[pl.ds(0, KG), pl.ds(0, 48), cols(src)], osem.at[s])
+        cp.start()
+        locs.append(cp)
     for cp in sends:
         cp.wait()
-    own.wait()
-
-
-def core_out(basis_t, tensor):
+    for cp in locs:
+        cp.wait()
+
+
+def core_out(basis_t, tensor, below, above, far):
     f = jnp.float32
     V, D = pltpu.VMEM, pltpu.SemaphoreType.DMA
     ng = len(GROUPS)
+    ANY = pl.BlockSpec(memory_space=pl.ANY)
     return pl.pallas_call(
         core_kernel,
         out_shape=jax.ShapeDtypeStruct((16, 48, 1024), f),
-        in_specs=[pl.BlockSpec(memory_space=pltpu.VMEM), pl.BlockSpec(memory_space=pl.ANY)],
-        out_specs=pl.BlockSpec(memory_space=pl.ANY),
-        scratch_shapes=[V((16, 512, 128), f), V((384, 512), jnp.bfloat16), V((384, 512), jnp.bfloat16), V((16, 384, 128), f),
-                        D((ng,)), D((7, ng)), D((7, ng)), D],
+        in_specs=[pl.BlockSpec(memory_space=pltpu.VMEM)] + [ANY] * 7,
+        out_specs=ANY,
+        scratch_shapes=[V((16 - KG, 512, 128), f), V((4, KG, 512, 128), f), V((384, 512), jnp.bfloat16), V((384, 512), jnp.bfloat16),
+                        V((16 - KG, 384, 128), f), V((4, 2, KG, 48, 128), f),
+                        D((ng,)), D((4, 2)), D((7, ng)), D((7, ng)), D((4,)), D((4,)), D((5,))],
         compiler_params=pltpu.CompilerParams(collective_id=1, has_side_effects=True, vmem_limit_bytes=62 << 20),
         name="core_out",
-    )(basis_t, tensor)
+    )(basis_t, tensor, *below, *above, *far)
+
+
+def shift(x, d):
+    pairs = [(zz * 2 + cc, ((zz + d) % 4) * 2 + cc) for zz in range(4) for cc in range(2)]
+    return lax.ppermute(x, "gy", pairs)
 
 
 def body(tensor, start_basis):
-    basis_t = qr(gram_sum(tensor), start_basis)
-    return core_out(basis_t, tensor)
+    half = KG // 2
+    parts = (tensor[:half], tensor[half:KG])
+    below = [shift(p, 1) for p in parts]
+    above = [shift(p, -1) for p in parts]
+    packed = gram_sum(tensor)
+    gram, basis_t = sweep_first(packed, start_basis)
+    gram, basis_t, below, above = lax.optimization_barrier((gram, basis_t, below, above))
+    far = (shift(below[0], 1), shift(above[1], -1))
+    basis_t = sweep_second(gram, basis_t)
+    return core_out(basis_t, tensor, below, above, far)
 
 
 def solution(mesh):

time: 121 us -> 147 us (1.21)
  Pallas kernels: 117 us -> 129 us
  starting transfers between devices: 0 us -> 10.2 us
  local copies, waits for them, and re-layouts: 3.97 us -> 7.01 us
    pallas_call x1, Pallas kernels: 31 us -> 58.5 us  [gram_sum(): pl.pallas_call(ar_kernel, out_shape=jax.ShapeDtypeStruct((160, 8, 128), f...]
    pallas_call x1, Pallas kernels: 39.3 us -> 24.1 us  [core_out(): pl.pallas_call(core_kernel, out_shape=jax.ShapeDtypeStruct((16, 48, 1024)...]
    ppermute x0 -> x6, starting transfers between devices: none -> 10.2 us  [shift(): return lax.ppermute(x, 'gy', pairs)]
    slice x0 -> x1, local copies, waits for them, and re-layouts: none -> 3.04 us  [body(): parts = (tensor[:half], tensor[half:KG])]
    pallas_call x1 -> x2, Pallas kernels: 46.6 us -> 46.4 us  [the longest x1 23.4 us: sweep_first(): pl.pallas_call(first_kernel, out_shape=(jax.ShapeDtypeStruct((512, 512),...]
    unnamed x1 -> x3, local copies, waits for them, and re-layouts: 3.97 us -> 3.97 us
  transfers between devices with their start and end apart: 0 -> 6, of which waited for: 0 -> 1; matrix products, arithmetic and copies ran while one was open for 0% -> 0% of each run, Pallas kernels for 0% -> 71%
where the time goes in v4:
time: 147 us
  Pallas kernels  129 us (88%)
  starting transfers between devices  10.2 us (7%)
  local copies, waits for them, and re-layouts  7.01 us (5%)
    pallas_call x1, Pallas kernels, gram_sum(): pl.pallas_call(ar_kernel, out_shape=jax.ShapeDtypeStruct((160, 8, 128), f...  58.5 us
    pallas_call x1, Pallas kernels, core_out(): pl.pallas_call(core_kernel, out_shape=jax.ShapeDtypeStruct((16, 48, 1024)...  24.1 us
    pallas_call x1, Pallas kernels, sweep_first(): pl.pallas_call(first_kernel, out_shape=(jax.ShapeDtypeStruct((512, 512),...  23.4 us
    pallas_call x1, Pallas kernels, sweep_second(): pl.pallas_call(second_kernel, out_shape=jax.ShapeDtypeStruct((384, 512),...  23 us
    ppermute x6, starting transfers between devices, shift(): return lax.ppermute(x, 'gy', pairs)  10.2 us
    unnamed x3, local copies, waits for them, and re-layouts  3.97 us
    slice x1, local copies, waits for them, and re-layouts, body(): parts = (tensor[:half], tensor[half:KG])  3.04 us
  transfers between devices with their start and end apart: 6, of which 1 were waited for; matrix products, arithmetic and copies ran while one was open for 0% of the time, Pallas kernels for 71%

profile of v4, /device:TPU:1, one launch (start us, length us, event | category | flops | bytes accessed | tf_op | source)
XLA Modules:
  0.0 146.7 jit_solution(3853759388127721732)
XLA Ops:
  0.0 3.0 %fusion = (f32[4,512,128]{2,1,0:T(8,128)}, f32[4,512,128]{2,1,0:T(8,128)}) fusion(f32[16,512,128]{2,1,0:T(8,128)} %t_ref.3), kind=kLoop, calls=%fused_computation | loop fusion | bytes 4194304 | tf_op jit(solution)/shard_map/slice | solution.py:359
  3.0 4.6 %collective-permute-start.3 = (f32[4,512,128]{2,1,0:T(8,128)}, f32[4,512,128]{2,1,0:T(8,128)S(1)}, u32[]{:S(2)}, u32[]{:S(2)}) collective-permute-start(f32[4,512,128]{2,1,0:T(8,128)} %get-tuple-element.21), channel_id=1, source_target_pairs={{0,6},{1,7},{2,0},{3,1},{4,2},{5,3},{6,4},{7,5},{8,14},{9,15},{10,... | collective-permute-start | bytes 3145736 | tf_op jit(solution)/shard_map/ppermute | solution.py:354
  7.6 0.0 collective-permute-start.1
  7.6 2.7 %collective-permute-start.2 = (f32[4,512,128]{2,1,0:T(8,128)}, f32[4,512,128]{2,1,0:T(8,128)}, u32[]{:S(2)}, u32[]{:S(2)}) collective-permute-start(f32[4,512,128]{2,1,0:T(8,128)} %get-tuple-element.22), channel_id=1, source_target_pairs={{0,6},{1,7},{2,0},{3,1},{4,2},{5,3},{6,4},{7,5},{8,14},{9,15},{10,... | collective-permute-start | bytes 3145736 | tf_op jit(solution)/shard_map/ppermute | solution.py:354
  10.3 0.0 collective-permute-start
  10.3 58.5 %gram_sum.1.p_ref = f32[160,8,128]{2,1,0:T(8,128)} custom-call(f32[16,512,128]{2,1,0:T(8,128)} %t_ref.3), custom_call_target="tpu_custom_call" | custom-call | tf_op jit(solution)/shard_map/gram_sum/pallas_call | solution.py:110
  68.8 23.4 %sweep_first.1 = (f32[512,512]{1,0:T(8,128)}, f32[384,512]{1,0:T(8,128)}) custom-call(f32[160,8,128]{2,1,0:T(8,128)} %gram_sum.1.p_ref, f32[512,384]{1,0:T(8,128)} %b_ref.1), custom_call_target="tpu_custom_call" | custom-call | flops 2000000000 | bytes 3000000 | tf_op jit(solution)/shard_map/sweep_first/pallas_call | solution.py:228
  92.1 0.0 collective-permute-done.3.g3b
  92.1 0.0 copy-start
  92.1 0.0 collective-permute-done.1.g1b
  92.2 0.0 collective-permute-done.2.g3a
  92.2 0.0 collective-permute-done.g1a
  92.2 0.3 collective-permute-start.4
  92.4 2.7 %collective-permute-start.5 = (f32[4,512,128]{2,1,0:T(8,128)S(1)}, f32[4,512,128]{2,1,0:T(8,128)}, u32[]{:S(2)}, u32[]{:S(2)}) collective-permute-start(f32[4,512,128]{2,1,0:T(8,128)S(1)} %collective-permute-done.3.g3b), channel_id=1, source_target_pairs={{0,6},{1,7},{2,0},{3,1},{4,2},{5,3},{6,4},{7,5},{8,14},{9,15},{10,... | collective-permute-start | bytes 3145736 | tf_op jit(solution)/shard_map/ppermute | solution.py:354
  95.1 23.0 %sweep_second.1.q_ref = f32[384,512]{1,0:T(8,128)} custom-call(f32[512,512]{1,0:T(8,128)} %get-tuple-element.15.g_ref, f32[384,512]{1,0:T(8,128)} %get-tuple-element.16.q_ref), custom_call_target="tpu_custom_call" | custom-call | flops 2000000000 | bytes 3000000 | tf_op jit(solution)/shard_map/sweep_second/pallas_call | solution.py:236
  118.1 0.5 collective-permute-done.4.g2a
  118.7 0.0 collective-permute-done.5.g2b
  118.7 0.0 copy-done
  118.7 24.1 %core_out.1 = f32[16,48,1024]{2,1,0:T(8,128)} custom-call(f32[384,512]{1,0:T(8,128)} %sweep_second.1.q_ref, f32[16,512,128]{2,1,0:T(8,128)} %t_ref.3, f32[4,512,128]{2,1,0:T(8,128)} %collective-permute-done.g1a, f32[4,512,128]{2,1,0:T(8,128)} %collective-permute-done.1.g1b, f32[4,512,128]{2,1,0:T(8,128)} %collective-permute-done.2.g3a, ...), custom_call_target="tpu_custom_call" | custom-call | tf_op jit(solution)/shard_map/core_out/pallas_call | solution.py:339
  142.8 4.0 %copy.4 = f32[16,48,1024]{2,1,0:T(8,128)} copy(f32[16,48,1024]{2,1,0:T(8,128)} %core_out.1) | data formatting | bytes 6291456
Async XLA Ops:
  3.0 89.1 %collective-permute-start.3 = (f32[4,512,128]{2,1,0:T(8,128)}, f32[4,512,128]{2,1,0:T(8,128)S(1)}, u32[]{:S(2)}, u32[]{:S(2)}) collective-permute-start(f32[4,512,128]{2,1,0:T(8,128)} %get-tuple-element.21), channel_id=1, source_target_pairs={{0,6},{1,7},{2,0},{3,1},{4,2},{5,3},{6,4},{7,5},{8,14},{9,15},{10,... | collective-permute-start | bytes 3145736 | tf_op jit(solution)/shard_map/ppermute | solution.py:354
  7.6 84.5 %collective-permute-start.1 = (f32[4,512,128]{2,1,0:T(8,128)}, f32[4,512,128]{2,1,0:T(8,128)}, u32[]{:S(2)}, u32[]{:S(2)}) collective-permute-start(f32[4,512,128]{2,1,0:T(8,128)} %get-tuple-element.21), channel_id=1, source_target_pairs={{0,2},{1,3},{2,4},{3,5},{4,6},{5,7},{6,0},{7,1},{8,10},{9,11},{10,... | collective-permute-start | bytes 3145736 | tf_op jit(solution)/shard_map/ppermute | solution.py:354
  7.6 84.5 %collective-permute-start.2 = (f32[4,512,128]{2,1,0:T(8,128)}, f32[4,512,128]{2,1,0:T(8,128)}, u32[]{:S(2)}, u32[]{:S(2)}) collective-permute-start(f32[4,512,128]{2,1,0:T(8,128)} %get-tuple-element.22), channel_id=1, source_target_pairs={{0,6},{1,7},{2,0},{3,1},{4,2},{5,3},{6,4},{7,5},{8,14},{9,15},{10,... | collective-permute-start | bytes 3145736 | tf_op jit(solution)/shard_map/ppermute | solution.py:354
  10.3 81.9 %collective-permute-start = (f32[4,512,128]{2,1,0:T(8,128)}, f32[4,512,128]{2,1,0:T(8,128)}, u32[]{:S(2)}, u32[]{:S(2)}) collective-permute-start(f32[4,512,128]{2,1,0:T(8,128)} %get-tuple-element.22), channel_id=1, source_target_pairs={{0,2},{1,3},{2,4},{3,5},{4,6},{5,7},{6,0},{7,1},{8,10},{9,11},{10,... | collective-permute-start | bytes 3145736 | tf_op jit(solution)/shard_map/ppermute | solution.py:354
  92.1 26.5 %copy-start = (f32[4,512,128]{2,1,0:T(8,128)}, f32[4,512,128]{2,1,0:T(8,128)S(1)}, u32[]{:S(2)}) copy-start(f32[4,512,128]{2,1,0:T(8,128)S(1)} %collective-permute-done.3.g3b) | copy-start | bytes 3145732
  92.2 26.5 %collective-permute-start.4 = (f32[4,512,128]{2,1,0:T(8,128)}, f32[4,512,128]{2,1,0:T(8,128)}, u32[]{:S(2)}, u32[]{:S(2)}) collective-permute-start(f32[4,512,128]{2,1,0:T(8,128)} %collective-permute-done.g1a), channel_id=1, source_target_pairs={{0,2},{1,3},{2,4},{3,5},{4,6},{5,7},{6,0},{7,1},{8,10},{9,11},{10,... | collective-permute-start | bytes 3145736 | tf_op jit(solution)/shard_map/ppermute | solution.py:354
  92.4 26.2 %collective-permute-start.5 = (f32[4,512,128]{2,1,0:T(8,128)S(1)}, f32[4,512,128]{2,1,0:T(8,128)}, u32[]{:S(2)}, u32[]{:S(2)}) collective-permute-start(f32[4,512,128]{2,1,0:T(8,128)S(1)} %collective-permute-done.3.g3b), channel_id=1, source_target_pairs={{0,6},{1,7},{2,0},{3,1},{4,2},{5,3},{6,4},{7,5},{8,14},{9,15},{10,... | collective-permute-start | bytes 3145736 | tf_op jit(solution)/shard_map/ppermute | solution.py:354

commit v5 on v3

--- a/solution.py
+++ b/solution.py
@@ -118,100 +118,155 @@
             V((5, 8, 128), f), V((4, 5, 8, 128), f), V((5, 8, 128), f),
             D((4,)), D((16,)), D((16,)), D((16,)), D((16,)), D((4,)), D((4,)), D((16,)), D((16,)), D((16,)), D((16,)),
         ],
-        compiler_params=pltpu.CompilerParams(collective_id=0, has_side_effects=True, vmem_limit_bytes=62 << 20),
+        compiler_params=pltpu.CompilerParams(collective_id=0, has_side_effects=True, vmem_limit_bytes=60 << 20),
         name="gram_sum",
     )(tensor)
 
 
-HI = lax.Precision.HIGHEST
+def split(x):
+    h = x.astype(jnp.bfloat16)
+    return h, (x - h.astype(jnp.float32)).astype(jnp.bfloat16)
+
+
 def mm(a, b, ca=1, cb=0):
-    return lax.dot_general(a, b, (((ca,), (cb,)), ((), ())), precision=HI, preferred_element_type=jnp.float32)
-
-def rep(x):
-    return jnp.broadcast_to(x, (8, 128))
-
-def chol_inv(D):
-    A = list(D)
+    ah, al = split(a)
+    bh, bl = split(b)
+
+    def dot(u, v):
+        return lax.dot_general(u, v, (((ca,), (cb,)), ((), ())), preferred_element_type=jnp.float32)
+
+    return dot(ah, bh) + (dot(ah, bl) + dot(al, bh))
+
+
+LOOK = 2
+
+
+def lanes(x, i):
+    return jnp.broadcast_to(x[:, i:i + 1], (8, 128))
+
+
+def rows(x, i):
+    return jnp.broadcast_to(x[i:i + 1, :], (8, 128))
+
+
+def chol_inv(A, one):
+    A = list(A)
     row = lax.broadcasted_iota(jnp.int32, (8, 128), 0)
     lane = lax.broadcasted_iota(jnp.int32, (8, 128), 1)
-    Z = [jnp.where(lane == row + 8 * g, 1.0, 0.0).astype(jnp.float32) for g in range(16)]
     out = []
+    C = [lanes(A[0], j) * one for j in range(8)]
     for p in range(16):
         c = 8 * p
-        S = [[rep(A[p][i:i+1, c+j:c+j+1]) for j in range(i+1)] for i in range(8)]
-        V = [rep(A[p][i:i+1, :]) for i in range(8)]
-        U = [rep(Z[p][i:i+1, :]) for i in range(8)]
-        L = [[None]*8 for _ in range(8)]
-        r = [None]*8
+        done = (lane >= c) & (lane < c + 8)
+        S = [[rows(C[j], i) for j in range(i + 1)] for i in range(8)]
+        top = jnp.where(done, jnp.where(lane == row + c, 1.0, 0.0), A[p])
+        V = [rows(top, i) for i in range(8)]
+        near = range(p + 1, min(p + 1 + LOOK, 16))
+        if p < 15:
+            C = [lanes(A[p + 1], c + 8 + j) for j in range(8)]
+        X = {g: [lanes(A[g], c + j) for j in range(8)] for g in range(p + 1, 16)}
+        for g in range(p + 1, 16):
+            A[g] = jnp.where(done, 0.0, A[g])
+        L = [[None] * 8 for _ in range(8)]
+        r = [None] * 8
         for j in range(8):
             r[j] = lax.rsqrt(S[j][j])
-            for i in range(j+1, 8):
+            for i in range(j + 1, 8):
                 L[i][j] = S[i][j] * r[j]
-            for i in range(j+1, 8):
-                for k in range(j+1, i+1):
+            for i in range(j + 1, 8):
+                for k in range(j + 1, i + 1):
                     S[i][k] = S[i][k] - L[i][j] * L[k][j]
             V[j] = V[j] * r[j]
-            U[j] = U[j] * r[j]
-            for i in range(j+1, 8):
+            for g in near:
+                x = X[g][j] * r[j]
+                for k in range(j + 1, 8):
+                    X[g][k] = X[g][k] - x * L[k][j]
+                A[g] = A[g] - x * V[j]
+                if g == p + 1:
+                    for k in range(8):
+                        C[k] = C[k] - x * rows(x, k)
+            for i in range(j + 1, 8):
                 V[i] = V[i] - L[i][j] * V[j]
-                U[i] = U[i] - L[i][j] * U[j]
-        o = U[0]
+        o = V[0]
         for i in range(1, 8):
-            o = jnp.where(row == i, U[i], o)
-        out.append(o)
-        if p == 15:
-            break
-        F = list(V); FU = list(U)
+            o = jnp.where(row == i, V[i], o)
+        out.append(jnp.where(lane < c + 8, o, 0.0))
+        if p + 1 + LOOK >= 16:
+            continue
+        F = list(V)
         for j in range(7, -1, -1):
             F[j] = F[j] * r[j]
-            FU[j] = FU[j] * r[j]
             for i in range(j):
                 F[i] = F[i] - L[j][i] * F[j]
-                FU[i] = FU[i] - L[j][i] * FU[j]
-        for g in range(p+1, 16):
-            X = [jnp.broadcast_to(A[g][:, c+j:c+j+1], (8, 128)) for j in range(8)]
-            def acc(Y, F):
-                t = [X[j]*F[j] for j in range(8)]
-                t = [t[0]+t[1], t[2]+t[3], t[4]+t[5], t[6]+t[7]]
-                return Y - ((t[0]+t[1]) + (t[2]+t[3]))
-            Z[g] = acc(Z[g], FU)
-            A[g] = acc(A[g], F)
+        for g in range(p + 1 + LOOK, 16):
+            t = [X[g][j] * F[j] for j in range(8)]
+            t = [t[0] + t[1], t[2] + t[3], t[4] + t[5], t[6] + t[7]]
+            A[g] = A[g] - ((t[0] + t[1]) + (t[2] + t[3]))
     return out
 
-def qr_kernel(p_ref, b_ref, o_ref, g_ref, pt, a, li):
+
+def sweep(pt, a, o_ref, li, one_ref):
+    one_ref[...] = jnp.ones((8, 128), jnp.float32)
+    a[...] = mm(pt[...], pt[...], 1, 1)
+
+    def block(kb, _):
+        k0 = pl.multiple_of(kb * 128, 128)
+        Li = chol_inv([a[pl.ds(k0 + 8 * g, 8), pl.ds(k0, 128)] for g in range(16)], one_ref[...])
+        for g in range(16):
+            li[8 * g:8 * g + 8, :] = Li[g]
+        for n in range(3):
+            @pl.when(kb == n)
+            def _():
+                lo, hi = 128 * n, 128 * n + 128
+                Q = mm(li[...], pt[lo:hi, :])
+                o_ref[lo:hi, :] = Q
+                if n < 2:
+                    R = mm(li[...], a[lo:hi, hi:])
+                    a[hi:, hi:] -= mm(R, R, 0, 0)
+                    pt[hi:, :] -= mm(R, Q, 0, 0)
+        return 0
+
+    lax.fori_loop(0, 3, block, 0)
+
+
+def first_kernel(p_ref, b_ref, g_ref, o_ref, pt, a, li, one):
     n = 0
     for i in range(4):
         for j in range(i + 1):
-            blk = p_ref[16*n:16*n+16].reshape(128, 128)
-            g_ref[128*i:128*i+128, 128*j:128*j+128] = blk
+            blk = p_ref[16 * n:16 * n + 16].reshape(128, 128)
+            g_ref[128 * i:128 * i + 128, 128 * j:128 * j + 128] = blk
             if j < i:
-                g_ref[128*j:128*j+128, 128*i:128*i+128] = blk.T
+                g_ref[128 * j:128 * j + 128, 128 * i:128 * i + 128] = blk.T
             n += 1
     pt[...] = mm(b_ref[...], g_ref[...], 0, 0)
-    def it(s, _):
-        @pl.when(s == 1)
-        def _():
-            pt[...] = mm(o_ref[...], g_ref[...])
-        a[...] = mm(pt[...], pt[...], 1, 1)
-        for kb in range(3):
-            k0 = kb*128
-            D = [a[k0+8*g:k0+8*g+8, k0:k0+128] for g in range(16)]
-            Li = chol_inv(D)
-            for g in range(16):
-                li[8*g:8*g+8, :] = Li[g]
-            Q = mm(li[...], pt[k0:k0+128, :])
-            o_ref[k0:k0+128, :] = Q
-            if kb < 2:
-                R = mm(li[...], a[k0:k0+128, k0+128:])
-                a[k0+128:, k0+128:] -= mm(R, R, 0, 0)
-                pt[k0+128:, :] -= mm(R, Q, 0, 0)
-        return 0
-    lax.fori_loop(0, 2, it, 0)
-
-def qr(G, B, **kw):
-    return pl.pallas_call(qr_kernel, out_shape=jax.ShapeDtypeStruct((384, 512), jnp.float32),
-        in_specs=[pl.BlockSpec(memory_space=pltpu.VMEM)]*2, out_specs=pl.BlockSpec(memory_space=pltpu.VMEM),
-        scratch_shapes=[pltpu.VMEM((512,512),jnp.float32), pltpu.VMEM((384,512),jnp.float32), pltpu.VMEM((384,384),jnp.float32), pltpu.VMEM((128,128),jnp.float32)], name="qr", **kw)(G, B)
+    sweep(pt, a, o_ref, li, one)
+
+
+def second_kernel(g_ref, q_ref, o_ref, pt, a, li, one):
+    pt[...] = mm(q_ref[...], g_ref[...])
+    sweep(pt, a, o_ref, li, one)
+
+
+SCRATCH = [pltpu.VMEM((384, 512), jnp.float32), pltpu.VMEM((384, 384), jnp.float32), pltpu.VMEM((128, 128), jnp.float32), pltpu.VMEM((8, 128), jnp.float32)]
+WHOLE = pl.BlockSpec(memory_space=pltpu.VMEM)
+SMALL = pltpu.CompilerParams(vmem_limit_bytes=16 << 20)
+COST = pl.CostEstimate(flops=2000000000, bytes_accessed=3000000, transcendentals=0)
+
+
+def sweep_first(packed, start):
+    return pl.pallas_call(
+        first_kernel,
+        out_shape=(jax.ShapeDtypeStruct((512, 512), jnp.float32), jax.ShapeDtypeStruct((384, 512), jnp.float32)),
+        in_specs=[WHOLE] * 2, out_specs=(WHOLE, WHOLE), scratch_shapes=SCRATCH, cost_estimate=COST, compiler_params=SMALL, name="sweep_first",
+    )(packed, start)
+
+
+def sweep_second(gram, basis_t):
+    return pl.pallas_call(
+        second_kernel,
+        out_shape=jax.ShapeDtypeStruct((384, 512), jnp.float32),
+        in_specs=[WHOLE] * 2, out_specs=WHOLE, scratch_shapes=SCRATCH, cost_estimate=COST, compiler_params=SMALL, name="sweep_second",
+    )(gram, basis_t)
 
 
 RELS = [(2, 0), (2, 1), (1, 0), (3, 0), (1, 1), (3, 1), (0, 1)]
@@ -277,16 +332,17 @@
         core_kernel,
         out_shape=jax.ShapeDtypeStruct((16, 48, 1024), f),
         in_specs=[pl.BlockSpec(memory_space=pltpu.VMEM), pl.BlockSpec(memory_space=pl.ANY)],
-        out_specs=pl.BlockSpec(memory_space=pl.ANY),
+        out_specs=pl.BlockSpec(memory_space=pltpu.VMEM),
         scratch_shapes=[V((16, 512, 128), f), V((384, 512), jnp.bfloat16), V((384, 512), jnp.bfloat16), V((16, 384, 128), f),
                         D((ng,)), D((7, ng)), D((7, ng)), D],
-        compiler_params=pltpu.CompilerParams(collective_id=1, has_side_effects=True, vmem_limit_bytes=62 << 20),
+        compiler_params=pltpu.CompilerParams(collective_id=1, has_side_effects=True, vmem_limit_bytes=24 << 20),
         name="core_out",
     )(basis_t, tensor)
 
 
 def body(tensor, start_basis):
-    basis_t = qr(gram_sum(tensor), start_basis)
+    gram, basis_t = sweep_first(gram_sum(tensor), start_basis)
+    basis_t = sweep_second(gram, basis_t)
     return core_out(basis_t, tensor)
 
 

time: 121 us -> 94.5 us (0.78)
  Pallas kernels: 117 us -> 91.5 us
  local copies, waits for them, and re-layouts: 3.97 us -> 2.76 us
    pallas_call x1 -> x2, Pallas kernels: 46.6 us -> 21.9 us  [the longest x1 11.1 us: sweep_first(): pl.pallas_call(first_kernel, out_shape=(jax.ShapeDtypeStruct((512, 512),...]
    unnamed x1 -> x7, local copies, waits for them, and re-layouts: 3.97 us -> 2.76 us
where the time goes in v5:
time: 94.5 us; the launch traced here: 94.3 us
  Pallas kernels  91.5 us (97%)
  local copies, waits for them, and re-layouts  2.76 us (3%)
    pallas_call x1, Pallas kernels, core_out(): pl.pallas_call(core_kernel, out_shape=jax.ShapeDtypeStruct((16, 48, 1024)...  38.4 us
    pallas_call x1, Pallas kernels, gram_sum(): pl.pallas_call(ar_kernel, out_shape=jax.ShapeDtypeStruct((160, 8, 128), f...  31.1 us
    pallas_call x1, Pallas kernels, sweep_first(): pl.pallas_call(first_kernel, out_shape=(jax.ShapeDtypeStruct((512, 512),...  11.1 us
    pallas_call x1, Pallas kernels, sweep_second(): pl.pallas_call(second_kernel, out_shape=jax.ShapeDtypeStruct((384, 512),...  10.8 us
    unnamed x7, local copies, waits for them, and re-layouts  2.76 us

profile of v5, /device:TPU:1, one launch (start us, length us, event | category | flops | bytes accessed | tf_op | source)
XLA Modules:
  0.0 94.3 jit_solution(2364195111388127516)
XLA Ops:
  0.0 0.0 copy-start.2
  0.0 31.1 %gram_sum.1.p_ref = f32[160,8,128]{2,1,0:T(8,128)} custom-call(f32[16,512,128]{2,1,0:T(8,128)} %t_ref.3), custom_call_target="tpu_custom_call" | custom-call | tf_op jit(solution)/shard_map/gram_sum/pallas_call | solution.py:110
  31.1 0.0 copy-done.2
  31.1 0.0 copy-start.1
  31.1 1.1 %copy-done.1 = f32[160,8,128]{2,1,0:T(8,128)S(1)} copy-done((f32[160,8,128]{2,1,0:T(8,128)S(1)}, f32[160,8,128]{2,1,0:T(8,128)}, u32[]{:S(2)}) %copy-start.1) | copy-done | bytes 655384
  32.2 11.1 %sweep_first.1 = (f32[512,512]{1,0:T(8,128)S(1)}, f32[384,512]{1,0:T(8,128)S(1)}) custom-call(f32[160,8,128]{2,1,0:T(8,128)S(1)} %copy-done.1, f32[512,384]{1,0:T(8,128)S(1)} %copy-done.2), custom_call_target="tpu_custom_call" | custom-call | flops 2000000000 | bytes 3000000 | tf_op jit(solution)/shard_map/sweep_first/pallas_call | solution.py:257
  43.3 0.0 copy-start
  43.4 10.8 %sweep_second.1.q_ref = f32[384,512]{1,0:T(8,128)S(1)} custom-call(f32[512,512]{1,0:T(8,128)S(1)} %get-tuple-element.7.g_ref, f32[384,512]{1,0:T(8,128)S(1)} %get-tuple-element.8.q_ref), custom_call_target="tpu_custom_call" | custom-call | flops 2000000000 | bytes 3000000 | tf_op jit(solution)/shard_map/sweep_second/pallas_call | solution.py:265
  54.2 0.0 copy-done
  54.2 38.4 %core_out.1 = f32[16,48,1024]{2,1,0:T(8,128)S(1)} custom-call(f32[384,512]{1,0:T(8,128)S(1)} %sweep_second.1.q_ref, f32[16,512,128]{2,1,0:T(8,128)S(1)} %copy-done), custom_call_target="tpu_custom_call" | custom-call | tf_op jit(solution)/shard_map/core_out/pallas_call | solution.py:331
  92.6 1.7 %copy.4 = f32[16,48,1024]{2,1,0:T(8,128)} copy(f32[16,48,1024]{2,1,0:T(8,128)S(1)} %core_out.1) | data formatting | bytes 6291456
Async XLA Ops:
  0.0 31.1 %copy-start.2 = (f32[512,384]{1,0:T(8,128)S(1)}, f32[512,384]{1,0:T(8,128)}, u32[]{:S(2)}) copy-start(f32[512,384]{1,0:T(8,128)} %b_ref.1) | copy-start | bytes 2359300
  31.1 1.1 %copy-start.1 = (f32[160,8,128]{2,1,0:T(8,128)S(1)}, f32[160,8,128]{2,1,0:T(8,128)}, u32[]{:S(2)}) copy-start(f32[160,8,128]{2,1,0:T(8,128)} %gram_sum.1.p_ref) | copy-start | bytes 1966084
  43.3 10.8 %copy-start = (f32[16,512,128]{2,1,0:T(8,128)S(1)}, f32[16,512,128]{2,1,0:T(8,128)}, u32[]{:S(2)}) copy-start(f32[16,512,128]{2,1,0:T(8,128)} %t_ref.3) | copy-start | bytes 12582916

commit v6 on v5

--- a/solution.py
+++ b/solution.py
@@ -32,6 +32,9 @@
     for d in range(1, 4):
         pl.semaphore_signal(barrier, inc=1, device_id=(gx, ((z + d) % 4) * 2 + c), device_id_type=MESH)
 
+    def dot(a, b):
+        return lax.dot_general(a, b, NT, preferred_element_type=jnp.float32)
+
     for i in range(4):
         loads[i].wait()
         for s in range(4 * i, 4 * i + 4):
@@ -39,17 +42,20 @@
             h = v.astype(BF)
             hb[:, 128 * s:128 * s + 128] = h
             lb[:, 128 * s:128 * s + 128] = (v - h.astype(jnp.float32)).astype(BF)
-
-    def dot(a, b):
-        return lax.dot_general(a, b, NT, preferred_element_type=jnp.float32)
-
-    for (r0, c0) in ((0, 0), (256, 0), (256, 256)):
-        hr, lr = hb[r0:r0 + 256, :], lb[r0:r0 + 256, :]
-        hc, lc = hb[c0:c0 + 256, :], lb[c0:c0 + 256, :]
-        g = dot(hr, hc) + dot(hr, lc) + dot(lr, hc)
-        for n, (i, j) in enumerate(BLOCKS):
-            if r0 <= 128 * i < r0 + 256 and c0 <= 128 * j < c0 + 256:
-                gp[16 * n:16 * n + 16] = g[128 * i - r0:128 * i - r0 + 128, 128 * j - c0:128 * j - c0 + 128].reshape(16, 8, 128)
+        if i % 2 == 0:
+            continue
+        ks = slice(1024 * (i // 2), 1024 * (i // 2) + 1024)
+        for (r0, c0) in ((0, 0), (256, 0), (256, 256)):
+            hr, lr = hb[r0:r0 + 256, ks], lb[r0:r0 + 256, ks]
+            hc, lc = hb[c0:c0 + 256, ks], lb[c0:c0 + 256, ks]
+            g = dot(hr, hc) + dot(hr, lc) + dot(lr, hc)
+            for n, (bi, bj) in enumerate(BLOCKS):
+                if r0 <= 128 * bi < r0 + 256 and c0 <= 128 * bj < c0 + 256:
+                    part = g[128 * bi - r0:128 * bi - r0 + 128, 128 * bj - c0:128 * bj - c0 + 128].reshape(16, 8, 128)
+                    if i == 1:
+                        gp[16 * n:16 * n + 16] = part
+                    else:
+                        gp[16 * n:16 * n + 16] += part
 
     pl.semaphore_wait(barrier, 19)
     pieces = lambda core, g: pl.ds(80 * core + 5 * g, 5)
@@ -149,11 +155,9 @@
     return jnp.broadcast_to(x[i:i + 1, :], (8, 128))
 
 
-def chol_inv(A, one):
-    A = list(A)
+def chol_steps(A, one, li):
     row = lax.broadcasted_iota(jnp.int32, (8, 128), 0)
     lane = lax.broadcasted_iota(jnp.int32, (8, 128), 1)
-    out = []
     C = [lanes(A[0], j) * one for j in range(8)]
     for p in range(16):
         c = 8 * p
@@ -190,7 +194,8 @@
         o = V[0]
         for i in range(1, 8):
             o = jnp.where(row == i, V[i], o)
-        out.append(jnp.where(lane < c + 8, o, 0.0))
+        li[c:c + 8, :] = jnp.where(lane < c + 8, o, 0.0)
+        yield
         if p + 1 + LOOK >= 16:
             continue
         F = list(V)
@@ -202,34 +207,21 @@
             t = [X[g][j] * F[j] for j in range(8)]
             t = [t[0] + t[1], t[2] + t[3], t[4] + t[5], t[6] + t[7]]
             A[g] = A[g] - ((t[0] + t[1]) + (t[2] + t[3]))
-    return out
-
-
-def sweep(pt, a, o_ref, li, one_ref):
-    one_ref[...] = jnp.ones((8, 128), jnp.float32)
-    a[...] = mm(pt[...], pt[...], 1, 1)
-
-    def block(kb, _):
-        k0 = pl.multiple_of(kb * 128, 128)
-        Li = chol_inv([a[pl.ds(k0 + 8 * g, 8), pl.ds(k0, 128)] for g in range(16)], one_ref[...])
-        for g in range(16):
-            li[8 * g:8 * g + 8, :] = Li[g]
-        for n in range(3):
-            @pl.when(kb == n)
-            def _():
-                lo, hi = 128 * n, 128 * n + 128
-                Q = mm(li[...], pt[lo:hi, :])
-                o_ref[lo:hi, :] = Q
-                if n < 2:
-                    R = mm(li[...], a[lo:hi, hi:])
-                    a[hi:, hi:] -= mm(R, R, 0, 0)
-                    pt[hi:, :] -= mm(R, Q, 0, 0)
-        return 0
-
-    lax.fori_loop(0, 3, block, 0)
-
-
-def first_kernel(p_ref, b_ref, g_ref, o_ref, pt, a, li, one):
+
+
+def groups(ref):
+    return [ref[8 * g:8 * g + 8, :] for g in range(16)]
+
+
+def run(*steps):
+    steps = list(steps)
+    while steps:
+        for one in list(steps):
+            if next(one, True) is True:
+                steps.remove(one)
+
+
+def sweeps_kernel(p_ref, b_ref, o_ref, g_ref, p, q, a, li, one_ref):
     n = 0
     for i in range(4):
         for j in range(i + 1):
@@ -238,35 +230,80 @@
             if j < i:
                 g_ref[128 * j:128 * j + 128, 128 * i:128 * i + 128] = blk.T
             n += 1
-    pt[...] = mm(b_ref[...], g_ref[...], 0, 0)
-    sweep(pt, a, o_ref, li, one)
-
-
-def second_kernel(g_ref, q_ref, o_ref, pt, a, li, one):
-    pt[...] = mm(q_ref[...], g_ref[...])
-    sweep(pt, a, o_ref, li, one)
-
-
-SCRATCH = [pltpu.VMEM((384, 512), jnp.float32), pltpu.VMEM((384, 384), jnp.float32), pltpu.VMEM((128, 128), jnp.float32), pltpu.VMEM((8, 128), jnp.float32)]
-WHOLE = pl.BlockSpec(memory_space=pltpu.VMEM)
-SMALL = pltpu.CompilerParams(vmem_limit_bytes=16 << 20)
-COST = pl.CostEstimate(flops=2000000000, bytes_accessed=3000000, transcendentals=0)
-
-
-def sweep_first(packed, start):
+    one_ref[...] = jnp.ones((8, 128), jnp.float32)
+    one = one_ref[...]
+    first, second = 0, 3
+
+    def product(s, k, source, cs):
+        p[s + k] = mm(source, g_ref[...], cs, 0)
+        for j in range(k + 1):
+            a[s + j, k] = mm(p[s + j], p[s + k], 1, 1)
+
+    def basis(s, k):
+        q[s + k] = mm(li[s + k], p[s + k])
+
+    def factor(s, k, j):
+        a[s + k, j] = mm(li[s + k], a[s + k, j])
+
+    def reduce_gram(s, k, i, j):
+        a[s + i, j] -= mm(a[s + k, i], a[s + k, j], 0, 0)
+
+    def reduce_product(s, k, j):
+        p[s + j] -= mm(a[s + k, j], q[s + k], 0, 0)
+
+    def chol(s, k):
+        return chol_steps(groups(a.at[s + k, k]), one, li.at[s + k])
+
+    for k in range(3):
+        product(first, k, b_ref[:, 128 * k:128 * k + 128], 0)
+    run(chol(first, 0))
+    factor(first, 0, 1)
+    reduce_gram(first, 0, 1, 1)
+    basis(first, 0)
+    product(second, 0, q[0], 1)
+    factor(first, 0, 2)
+    reduce_gram(first, 0, 1, 2)
+    reduce_gram(first, 0, 2, 2)
+    reduce_product(first, 0, 1)
+    reduce_product(first, 0, 2)
+    run(chol(first, 1), chol(second, 0))
+    factor(first, 1, 2)
+    reduce_gram(first, 1, 2, 2)
+    basis(first, 1)
+    product(second, 1, q[1], 1)
+    factor(second, 0, 1)
+    reduce_gram(second, 0, 1, 1)
+    reduce_product(first, 1, 2)
+    basis(second, 0)
+    reduce_product(second, 0, 1)
+    run(chol(first, 2), chol(second, 1))
+    basis(first, 2)
+    product(second, 2, q[2], 1)
+    factor(second, 0, 2)
+    reduce_gram(second, 0, 2, 2)
+    factor(second, 1, 2)
+    reduce_gram(second, 1, 2, 2)
+    basis(second, 1)
+    reduce_product(second, 0, 2)
+    reduce_product(second, 1, 2)
+    run(chol(second, 2))
+    basis(second, 2)
+    for k in range(3):
+        o_ref[128 * k:128 * k + 128, :] = q[3 + k]
+
+
+def sweeps(packed, start):
+    f = jnp.float32
+    whole = pl.BlockSpec(memory_space=pltpu.VMEM)
     return pl.pallas_call(
-        first_kernel,
-        out_shape=(jax.ShapeDtypeStruct((512, 512), jnp.float32), jax.ShapeDtypeStruct((384, 512), jnp.float32)),
-        in_specs=[WHOLE] * 2, out_specs=(WHOLE, WHOLE), scratch_shapes=SCRATCH, cost_estimate=COST, compiler_params=SMALL, name="sweep_first",
+        sweeps_kernel,
+        out_shape=jax.ShapeDtypeStruct((384, 512), f),
+        in_specs=[whole] * 2, out_specs=whole,
+        scratch_shapes=[pltpu.VMEM((512, 512), f), pltpu.VMEM((6, 128, 512), f), pltpu.VMEM((6, 128, 512), f),
+                        pltpu.VMEM((6, 3, 128, 128), f), pltpu.VMEM((6, 128, 128), f), pltpu.VMEM((8, 128), f)],
+        cost_estimate=pl.CostEstimate(flops=4000000000, bytes_accessed=3000000, transcendentals=0),
+        compiler_params=pltpu.CompilerParams(vmem_limit_bytes=24 << 20), name="sweeps",
     )(packed, start)
-
-
-def sweep_second(gram, basis_t):
-    return pl.pallas_call(
-        second_kernel,
-        out_shape=jax.ShapeDtypeStruct((384, 512), jnp.float32),
-        in_specs=[WHOLE] * 2, out_specs=WHOLE, scratch_shapes=SCRATCH, cost_estimate=COST, compiler_params=SMALL, name="sweep_second",
-    )(gram, basis_t)
 
 
 RELS = [(2, 0), (2, 1), (1, 0), (3, 0), (1, 1), (3, 1), (0, 1)]
@@ -341,9 +378,7 @@
 
 
 def body(tensor, start_basis):
-    gram, basis_t = sweep_first(gram_sum(tensor), start_basis)
-    basis_t = sweep_second(gram, basis_t)
-    return core_out(basis_t, tensor)
+    return core_out(sweeps(gram_sum(tensor), start_basis), tensor)
 
 
 def solution(mesh):

time: 94.5 us -> 92.3 us (0.977)
  Pallas kernels: 91.5 us -> 89.4 us
    pallas_call x2 -> x1, Pallas kernels: 21.9 us -> 18.8 us  [sweeps(): pl.pallas_call(sweeps_kernel, out_shape=jax.ShapeDtypeStruct((384, 512),...]
where the time goes in v6:
time: 92.3 us; the launch traced here: 92.2 us
  Pallas kernels  89.4 us (97%)
  local copies, waits for them, and re-layouts  2.75 us (3%)
    pallas_call x1, Pallas kernels, core_out(): pl.pallas_call(core_kernel, out_shape=jax.ShapeDtypeStruct((16, 48, 1024)...  38.7 us
    pallas_call x1, Pallas kernels, gram_sum(): pl.pallas_call(ar_kernel, out_shape=jax.ShapeDtypeStruct((160, 8, 128), f...  31.9 us
    pallas_call x1, Pallas kernels, sweeps(): pl.pallas_call(sweeps_kernel, out_shape=jax.ShapeDtypeStruct((384, 512),...  18.8 us
    unnamed x7, local copies, waits for them, and re-layouts  2.75 us

profile of v6, /device:TPU:1, one launch (start us, length us, event | category | flops | bytes accessed | tf_op | source)
XLA Modules:
  0.0 92.2 jit_solution(385104467484385882)
XLA Ops:
  0.0 0.0 copy-start.2
  0.0 31.9 %gram_sum.1.p_ref = f32[160,8,128]{2,1,0:T(8,128)} custom-call(f32[16,512,128]{2,1,0:T(8,128)} %t_ref.3), custom_call_target="tpu_custom_call" | custom-call | tf_op jit(solution)/shard_map/gram_sum/pallas_call | solution.py:116
  31.9 0.0 copy-done.2
  31.9 0.0 copy-start.1
  31.9 1.1 %copy-done.1 = f32[160,8,128]{2,1,0:T(8,128)S(1)} copy-done((f32[160,8,128]{2,1,0:T(8,128)S(1)}, f32[160,8,128]{2,1,0:T(8,128)}, u32[]{:S(2)}) %copy-start.1) | copy-done | bytes 655384
  33.0 0.0 copy-start
  33.0 18.8 %sweeps.1.q_ref = f32[384,512]{1,0:T(8,128)S(1)} custom-call(f32[160,8,128]{2,1,0:T(8,128)S(1)} %copy-done.1, f32[512,384]{1,0:T(8,128)S(1)} %copy-done.2), custom_call_target="tpu_custom_call" | custom-call | flops 4000000000 | bytes 3000000 | tf_op jit(solution)/shard_map/sweeps/pallas_call | solution.py:298
  51.8 0.0 copy-done
  51.8 38.7 %core_out.1 = f32[16,48,1024]{2,1,0:T(8,128)S(1)} custom-call(f32[384,512]{1,0:T(8,128)S(1)} %sweeps.1.q_ref, f32[16,512,128]{2,1,0:T(8,128)S(1)} %copy-done), custom_call_target="tpu_custom_call" | custom-call | tf_op jit(solution)/shard_map/core_out/pallas_call | solution.py:368
  90.5 1.7 %copy.4 = f32[16,48,1024]{2,1,0:T(8,128)} copy(f32[16,48,1024]{2,1,0:T(8,128)S(1)} %core_out.1) | data formatting | bytes 6291456
Async XLA Ops:
  0.0 31.9 %copy-start.2 = (f32[512,384]{1,0:T(8,128)S(1)}, f32[512,384]{1,0:T(8,128)}, u32[]{:S(2)}) copy-start(f32[512,384]{1,0:T(8,128)} %b_ref.1) | copy-start | bytes 2359300
  31.9 1.1 %copy-start.1 = (f32[160,8,128]{2,1,0:T(8,128)S(1)}, f32[160,8,128]{2,1,0:T(8,128)}, u32[]{:S(2)}) copy-start(f32[160,8,128]{2,1,0:T(8,128)} %gram_sum.1.p_ref) | copy-start | bytes 1966084
  33.0 18.8 %copy-start = (f32[16,512,128]{2,1,0:T(8,128)S(1)}, f32[16,512,128]{2,1,0:T(8,128)}, u32[]{:S(2)}) copy-start(f32[16,512,128]{2,1,0:T(8,128)} %t_ref.3) | copy-start | bytes 12582916

commit v7 on v6

--- a/solution.py
+++ b/solution.py
@@ -12,7 +12,7 @@
 NT = (((1,), (1,)), ((), ()))
 
 
-def ar_kernel(t_ref, o_ref, tbuf, hb, lb, gp, ra, aa, rb, ab, rc, ac, tsem, sa, qa, sb, qb, sc, qc, sd, qd, se, qe):
+def ar_kernel(t_ref, o_ref, early_ref, tbuf, hb, lb, gp, ra, aa, rb, ab, rc, ac, tsem, sa, qa, sb, qb, sc, qc, sd, qd, se, qe, esem):
     gx = lax.axis_index("gx")
     gy = lax.axis_index("gy")
     x, y, z, c = gx // 4, gx % 4, gy // 2, gy % 2
@@ -31,9 +31,6 @@
         pl.semaphore_signal(barrier, inc=1, device_id=(plane(k, 1), gy), device_id_type=MESH)
     for d in range(1, 4):
         pl.semaphore_signal(barrier, inc=1, device_id=(gx, ((z + d) % 4) * 2 + c), device_id_type=MESH)
-
-    def dot(a, b):
-        return lax.dot_general(a, b, NT, preferred_element_type=jnp.float32)
 
     for i in range(4):
         loads[i].wait()
@@ -42,20 +39,20 @@
             h = v.astype(BF)
             hb[:, 128 * s:128 * s + 128] = h
             lb[:, 128 * s:128 * s + 128] = (v - h.astype(jnp.float32)).astype(BF)
-        if i % 2 == 0:
-            continue
-        ks = slice(1024 * (i // 2), 1024 * (i // 2) + 1024)
-        for (r0, c0) in ((0, 0), (256, 0), (256, 256)):
-            hr, lr = hb[r0:r0 + 256, ks], lb[r0:r0 + 256, ks]
-            hc, lc = hb[c0:c0 + 256, ks], lb[c0:c0 + 256, ks]
-            g = dot(hr, hc) + dot(hr, lc) + dot(lr, hc)
-            for n, (bi, bj) in enumerate(BLOCKS):
-                if r0 <= 128 * bi < r0 + 256 and c0 <= 128 * bj < c0 + 256:
-                    part = g[128 * bi - r0:128 * bi - r0 + 128, 128 * bj - c0:128 * bj - c0 + 128].reshape(16, 8, 128)
-                    if i == 1:
-                        gp[16 * n:16 * n + 16] = part
-                    else:
-                        gp[16 * n:16 * n + 16] += part
+
+    keep = pltpu.make_async_copy(tbuf.at[pl.ds(0, KG)], early_ref, esem)
+    keep.start()
+
+    def dot(a, b):
+        return lax.dot_general(a, b, NT, preferred_element_type=jnp.float32)
+
+    for (r0, c0) in ((0, 0), (256, 0), (256, 256)):
+        hr, lr = hb[r0:r0 + 256, :], lb[r0:r0 + 256, :]
+        hc, lc = hb[c0:c0 + 256, :], lb[c0:c0 + 256, :]
+        g = dot(hr, hc) + dot(hr, lc) + dot(lr, hc)
+        for n, (i, j) in enumerate(BLOCKS):
+            if r0 <= 128 * i < r0 + 256 and c0 <= 128 * j < c0 + 256:
+                gp[16 * n:16 * n + 16] = g[128 * i - r0:128 * i - r0 + 128, 128 * j - c0:128 * j - c0 + 128].reshape(16, 8, 128)
 
     pl.semaphore_wait(barrier, 19)
     pieces = lambda core, g: pl.ds(80 * core + 5 * g, 5)
@@ -106,6 +103,7 @@
         E.append(cp)
     for cp in E:
         cp.wait_recv()
+    keep.wait()
     for cp in A + B + C + D + E:
         cp.wait_send()
 
@@ -115,18 +113,21 @@
     V, D = pltpu.VMEM, pltpu.SemaphoreType.DMA
     return pl.pallas_call(
         ar_kernel,
-        out_shape=jax.ShapeDtypeStruct((160, 8, 128), f),
+        out_shape=(jax.ShapeDtypeStruct((160, 8, 128), f), jax.ShapeDtypeStruct((KG, 512, 128), f)),
         in_specs=[pl.BlockSpec(memory_space=pl.ANY)],
-        out_specs=pl.BlockSpec(memory_space=pltpu.VMEM),
+        out_specs=(pl.BlockSpec(memory_space=pltpu.VMEM), pl.BlockSpec(memory_space=pl.ANY)),
         scratch_shapes=[
             V((16, 512, 128), f), V((512, 2048), BF), V((512, 2048), BF),
             V((160, 8, 128), f), V((16, 5, 8, 128), f), V((16, 5, 8, 128), f), V((16, 5, 8, 128), f),
             V((5, 8, 128), f), V((4, 5, 8, 128), f), V((5, 8, 128), f),
-            D((4,)), D((16,)), D((16,)), D((16,)), D((16,)), D((4,)), D((4,)), D((16,)), D((16,)), D((16,)), D((16,)),
+            D((4,)), D((16,)), D((16,)), D((16,)), D((16,)), D((4,)), D((4,)), D((16,)), D((16,)), D((16,)), D((16,)), D,
         ],
         compiler_params=pltpu.CompilerParams(collective_id=0, has_side_effects=True, vmem_limit_bytes=60 << 20),
         name="gram_sum",
     )(tensor)
+
+
+KG = 2
 
 
 def split(x):
@@ -221,7 +222,21 @@
                 steps.remove(one)
 
 
-def sweeps_kernel(p_ref, b_ref, o_ref, g_ref, p, q, a, li, one_ref):
+def sweeps_kernel(p_ref, b_ref, t_ref, o_ref, below, above, far, g_ref, p, q, a, li, one_ref, ssem, rsem):
+    gx = lax.axis_index("gx")
+    gy = lax.axis_index("gy")
+    up, down = (gy + 2) % 8, (gy + 6) % 8
+    barrier = pltpu.get_barrier_semaphore()
+    for dev in (up, down):
+        pl.semaphore_signal(barrier, inc=1, device_id=(gx, dev), device_id_type=pl.DeviceIdType.MESH)
+    moves = []
+
+    def move(src, dst, dev):
+        n = len(moves)
+        cp = pltpu.make_async_remote_copy(src_ref=src, dst_ref=dst, send_sem=ssem.at[n], recv_sem=rsem.at[n], device_id=(gx, dev), device_id_type=pl.DeviceIdType.MESH)
+        cp.start()
+        moves.append(cp)
+
     n = 0
     for i in range(4):
         for j in range(i + 1):
@@ -230,6 +245,10 @@
             if j < i:
                 g_ref[128 * j:128 * j + 128, 128 * i:128 * i + 128] = blk.T
             n += 1
+    pl.semaphore_wait(barrier, 2)
+    for n in range(KG):
+        move(t_ref.at[n], below.at[n], up)
+        move(t_ref.at[KG - 1 - n], above.at[KG - 1 - n], down)
     one_ref[...] = jnp.ones((8, 128), jnp.float32)
     one = one_ref[...]
     first, second = 0, 3
@@ -276,6 +295,11 @@
     reduce_product(first, 1, 2)
     basis(second, 0)
     reduce_product(second, 0, 1)
+    for n in range(KG // 2):
+        moves[2 * n].wait_recv()
+        moves[2 * n + 1].wait_recv()
+        move(below.at[n], far.at[n], up)
+        move(above.at[KG - 1 - n], far.at[KG - 1 - n], down)
     run(chol(first, 2), chol(second, 1))
     basis(first, 2)
     product(second, 2, q[2], 1)
@@ -290,27 +314,34 @@
     basis(second, 2)
     for k in range(3):
         o_ref[128 * k:128 * k + 128, :] = q[3 + k]
-
-
-def sweeps(packed, start):
+    for n, cp in enumerate(moves):
+        cp.wait_send()
+        if n >= KG:
+            cp.wait_recv()
+
+
+def sweeps(packed, start, tensor):
     f = jnp.float32
     whole = pl.BlockSpec(memory_space=pltpu.VMEM)
+    anywhere = pl.BlockSpec(memory_space=pl.ANY)
     return pl.pallas_call(
         sweeps_kernel,
-        out_shape=jax.ShapeDtypeStruct((384, 512), f),
-        in_specs=[whole] * 2, out_specs=whole,
+        out_shape=(jax.ShapeDtypeStruct((384, 512), f),) + (jax.ShapeDtypeStruct((KG, 512, 128), f),) * 3,
+        in_specs=[whole] * 2 + [anywhere], out_specs=(whole,) + (anywhere,) * 3,
         scratch_shapes=[pltpu.VMEM((512, 512), f), pltpu.VMEM((6, 128, 512), f), pltpu.VMEM((6, 128, 512), f),
-                        pltpu.VMEM((6, 3, 128, 128), f), pltpu.VMEM((6, 128, 128), f), pltpu.VMEM((8, 128), f)],
+                        pltpu.VMEM((6, 3, 128, 128), f), pltpu.VMEM((6, 128, 128), f), pltpu.VMEM((8, 128), f),
+                        pltpu.SemaphoreType.DMA((3 * KG,)), pltpu.SemaphoreType.DMA((3 * KG,))],
         cost_estimate=pl.CostEstimate(flops=4000000000, bytes_accessed=3000000, transcendentals=0),
-        compiler_params=pltpu.CompilerParams(vmem_limit_bytes=24 << 20), name="sweeps",
-    )(packed, start)
+        compiler_params=pltpu.CompilerParams(collective_id=2, has_side_effects=True, vmem_limit_bytes=24 << 20), name="sweeps",
+    )(packed, start, tensor)
 
 
 RELS = [(2, 0), (2, 1), (1, 0), (3, 0), (1, 1), (3, 1), (0, 1)]
-GROUPS = [(0, 2), (2, 4), (4, 8), (8, 12), (12, 16)]
-
-
-def core_kernel(q_ref, t_ref, o_ref, tbuf, qh, ql, y, tsem, ssem, rsem, osem):
+KG = 2
+GROUPS = [(0, 2), (2, 4), (4, 8), (8, 14)]
+
+
+def core_kernel(q_ref, t_ref, g1, g3, g2, o_ref, tbuf, gbuf, qh, ql, y, yg, tsem, gsem, ssem, rsem, xsem, wsem, osem):
     gx = lax.axis_index("gx")
     gy = lax.axis_index("gy")
     z, c = gy // 2, gy % 2
@@ -319,9 +350,14 @@
         dz, dc = RELS[r]
         return ((z + dz) % 4) * 2 + (c + dc) % 2
 
-    loads = [pltpu.make_async_copy(t_ref.at[pl.ds(a, b - a)], tbuf.at[pl.ds(a, b - a)], tsem.at[n]) for n, (a, b) in enumerate(GROUPS)]
+    na = 16 - KG
+    loads = [pltpu.make_async_copy(t_ref.at[pl.ds(KG + a, b - a)], tbuf.at[pl.ds(a, b - a)], tsem.at[n]) for n, (a, b) in enumerate(GROUPS)]
+    gloads = [[pltpu.make_async_copy(r, gbuf.at[s], gsem.at[s])] for s, r in enumerate((t_ref.at[pl.ds(0, KG)], g1, g3, g2))]
     for cp in loads:
         cp.start()
+    for cps in gloads:
+        for cp in cps:
+            cp.start()
     barrier = pltpu.get_barrier_semaphore()
     for r in range(7):
         pl.semaphore_signal(barrier, inc=1, device_id=(gx, other(r)), device_id_type=pl.DeviceIdType.MESH)
@@ -333,14 +369,18 @@
     def dot(a, b):
         return jnp.dot(a, b, preferred_element_type=jnp.float32)
 
-    spot = pl.ds(pl.multiple_of(gy * 128, 128), 128)
+    def split(v):
+        th = v.astype(jnp.bfloat16)
+        return th, (v - th.astype(jnp.float32)).astype(jnp.bfloat16)
+
+    def cols(dev):
+        return pl.ds(pl.multiple_of(dev * 128, 128), 128)
+
     sends = []
     for n, (a, b) in enumerate(GROUPS):
         loads[n].wait()
         for k in range(a, b, 2):
-            v = jnp.concatenate([tbuf[k], tbuf[k + 1]], axis=1)
-            th = v.astype(jnp.bfloat16)
-            tl = (v - th.astype(jnp.float32)).astype(jnp.bfloat16)
+            th, tl = split(jnp.concatenate([tbuf[k], tbuf[k + 1]], axis=1))
             out = dot(qh[...], th) + dot(qh[...], tl) + dot(ql[...], th)
             y[k] = out[:, :128]
             y[k + 1] = out[:, 128:]
@@ -349,36 +389,64 @@
         for r in range(7):
             cp = pltpu.make_async_remote_copy(
                 src_ref=y.at[pl.ds(a, b - a), pl.ds(pl.multiple_of(48 * other(r), 8), 48)],
-                dst_ref=o_ref.at[pl.ds(a, b - a), pl.ds(0, 48), spot],
+                dst_ref=o_ref.at[pl.ds(KG + a, b - a), pl.ds(0, 48), cols(gy)],
                 send_sem=ssem.at[r, n], recv_sem=rsem.at[r, n],
                 device_id=(gx, other(r)), device_id_type=pl.DeviceIdType.MESH)
             cp.start()
             sends.append(cp)
-    own = pltpu.make_async_copy(y.at[pl.ds(0, 16), pl.ds(pl.multiple_of(48 * gy, 8), 48)], o_ref.at[pl.ds(0, 16), pl.ds(0, 48), spot], osem)
+    own = pltpu.make_async_copy(y.at[pl.ds(0, na), pl.ds(pl.multiple_of(48 * gy, 8), 48)], o_ref.at[pl.ds(KG, na), pl.ds(0, 48), cols(gy)], osem.at[4])
     own.start()
+    rows = pl.ds(pl.multiple_of(96 * z, 32), 96)
+    q2 = jnp.concatenate([qh[rows, :], ql[rows, :]], axis=0)
+    locs = [own]
+    for s, dz in enumerate((0, 3, 1, 2)):
+        for cp in gloads[s]:
+            cp.wait()
+        for k in range(0, KG, 2):
+            th, tl = split(jnp.concatenate([gbuf[s, k], gbuf[s, k + 1]], axis=1))
+            o2 = dot(q2, th)
+            out = o2[:96] + o2[96:] + dot(q2[:96], tl)
+            for d in range(2):
+                yg[s, 0, k + d] = out[:48, 128 * d:128 * d + 128]
+                yg[s, 1, k + d] = out[48:, 128 * d:128 * d + 128]
+        src = ((z + dz) % 4) * 2 + c
+        cp = pltpu.make_async_remote_copy(
+            src_ref=yg.at[s, 1 - c], dst_ref=o_ref.at[pl.ds(0, KG), pl.ds(0, 48), cols(src)],
+            send_sem=xsem.at[s], recv_sem=wsem.at[s],
+            device_id=(gx, z * 2 + 1 - c), device_id_type=pl.DeviceIdType.MESH)
+        cp.start()
+        sends.append(cp)
+        cp = pltpu.make_async_copy(yg.at[s, c], o_ref.at[pl.ds(0, KG), pl.ds(0, 48), cols(src)], osem.at[s])
+        cp.start()
+        locs.append(cp)
     for cp in sends:
         cp.wait()
-    own.wait()
-
-
-def core_out(basis_t, tensor):
+    for cp in locs:
+        cp.wait()
+
+
+def core_out(basis_t, tensor, below, above, far):
     f = jnp.float32
     V, D = pltpu.VMEM, pltpu.SemaphoreType.DMA
     ng = len(GROUPS)
+    ANY = pl.BlockSpec(memory_space=pl.ANY)
     return pl.pallas_call(
         core_kernel,
         out_shape=jax.ShapeDtypeStruct((16, 48, 1024), f),
-        in_specs=[pl.BlockSpec(memory_space=pltpu.VMEM), pl.BlockSpec(memory_space=pl.ANY)],
+        in_specs=[pl.BlockSpec(memory_space=pltpu.VMEM)] + [ANY] * 4,
         out_specs=pl.BlockSpec(memory_space=pltpu.VMEM),
-        scratch_shapes=[V((16, 512, 128), f), V((384, 512), jnp.bfloat16), V((384, 512), jnp.bfloat16), V((16, 384, 128), f),
-                        D((ng,)), D((7, ng)), D((7, ng)), D],
+        scratch_shapes=[V((16 - KG, 512, 128), f), V((4, KG, 512, 128), f), V((384, 512), jnp.bfloat16), V((384, 512), jnp.bfloat16),
+                        V((16 - KG, 384, 128), f), V((4, 2, KG, 48, 128), f),
+                        D((ng,)), D((4,)), D((7, ng)), D((7, ng)), D((4,)), D((4,)), D((5,))],
         compiler_params=pltpu.CompilerParams(collective_id=1, has_side_effects=True, vmem_limit_bytes=24 << 20),
         name="core_out",
-    )(basis_t, tensor)
+    )(basis_t, tensor, below, above, far)
 
 
 def body(tensor, start_basis):
-    return core_out(sweeps(gram_sum(tensor), start_basis), tensor)
+    packed, early = gram_sum(tensor)
+    basis_t, below, above, far = sweeps(packed, start_basis, early)
+    return core_out(basis_t, tensor, below, above, far)
 
 
 def solution(mesh):

time: 92.3 us -> 95.3 us (1.033)
  Pallas kernels: 89.4 us -> 91.2 us
  local copies, waits for them, and re-layouts: 2.75 us -> 3.8 us
    pallas_call x2, Pallas kernels: 50.7 us -> 55.9 us  [the longest x1 31.1 us: gram_sum(): pl.pallas_call(ar_kernel, out_shape=(jax.ShapeDtypeStruct((160, 8, 128),...]
    pallas_call x1, Pallas kernels: 38.7 us -> 35.3 us  [core_out(): pl.pallas_call(core_kernel, out_shape=jax.ShapeDtypeStruct((16, 48, 1024)...]
    unnamed x7 -> x9, local copies, waits for them, and re-layouts: 2.75 us -> 3.8 us
where the time goes in v7:
time: 95.3 us; the launch traced here: 95.1 us
  Pallas kernels  91.2 us (96%)
  local copies, waits for them, and re-layouts  3.8 us (4%)
    pallas_call x1, Pallas kernels, core_out(): pl.pallas_call(core_kernel, out_shape=jax.ShapeDtypeStruct((16, 48, 1024)...  35.3 us
    pallas_call x1, Pallas kernels, gram_sum(): pl.pallas_call(ar_kernel, out_shape=(jax.ShapeDtypeStruct((160, 8, 128),...  31.1 us
    pallas_call x1, Pallas kernels, sweeps(): pl.pallas_call(sweeps_kernel, out_shape=(jax.ShapeDtypeStruct((384, 512),...  24.8 us
    unnamed x9, local copies, waits for them, and re-layouts  3.8 us

profile of v7, /device:TPU:1, one launch (start us, length us, event | category | flops | bytes accessed | tf_op | source)
XLA Modules:
  0.0 95.1 jit_solution(11645070072277826423)
XLA Ops:
  0.0 0.0 copy-start.1
  0.0 31.1 %gram_sum.1 = (f32[160,8,128]{2,1,0:T(8,128)}, f32[2,512,128]{2,1,0:T(8,128)}) custom-call(f32[16,512,128]{2,1,0:T(8,128)} %t_ref.3), custom_call_target="tpu_custom_call" | custom-call | tf_op jit(solution)/shard_map/gram_sum/pallas_call | solution.py:114
  31.1 0.0 copy-done.1
  31.2 0.0 copy-start.2
  31.2 1.1 %copy-done.2 = f32[160,8,128]{2,1,0:T(8,128)S(1)} copy-done((f32[160,8,128]{2,1,0:T(8,128)S(1)}, f32[160,8,128]{2,1,0:T(8,128)}, u32[]{:S(2)}) %copy-start.2) | copy-done | bytes 655384
  32.2 0.0 copy-start.3
  32.2 1.0 %copy-done.3 = f32[2,512,128]{2,1,0:T(8,128)S(1)} copy-done((f32[2,512,128]{2,1,0:T(8,128)S(1)}, f32[2,512,128]{2,1,0:T(8,128)}, u32[]{:S(2)}) %copy-start.3) | copy-done | bytes 524312
  33.3 0.0 copy-start
  33.3 24.8 %sweeps.1 = (f32[384,512]{1,0:T(8,128)S(1)}, f32[2,512,128]{2,1,0:T(8,128)S(1)}, f32[2,512,128]{2,1,0:T(8,128)S(1)}, f32[2,512,128]{2,1,0:T(8,128)S(1)}) custom-call(f32[160,8,128]{2,1,0:T(8,128)S(1)} %copy-done.2, f32[512,384]{1,0:T(8,128)S(1)} %copy-done.1, f32[2,512,128]{2,1,0:T(8,128)S(1)} %copy-done.3), custom_call_target="tpu_custom_call" | custom-call | flops 4000000000 | bytes 3000000 | tf_op jit(solution)/shard_map/sweeps/pallas_call | solution.py:327
  58.0 0.0 copy-done
  58.1 35.3 %core_out.1 = f32[16,48,1024]{2,1,0:T(8,128)S(1)} custom-call(f32[384,512]{1,0:T(8,128)S(1)} %get-tuple-element.13.q_ref, f32[16,512,128]{2,1,0:T(8,128)S(1)} %copy-done, f32[2,512,128]{2,1,0:T(8,128)S(1)} %get-tuple-element.14.g1, f32[2,512,128]{2,1,0:T(8,128)S(1)} %get-tuple-element.15.g3, f32[2,512,128]{2,1,0:T(8,128)S(1)} %get-tuple-element.16.g2), custom_call_target="tpu_custom_call" | custom-call | tf_op jit(solution)/shard_map/core_out/pallas_call | solution.py:433
  93.4 1.7 %copy.4 = f32[16,48,1024]{2,1,0:T(8,128)} copy(f32[16,48,1024]{2,1,0:T(8,128)S(1)} %core_out.1) | data formatting | bytes 6291456
Async XLA Ops:
  0.0 31.1 %copy-start.1 = (f32[512,384]{1,0:T(8,128)S(1)}, f32[512,384]{1,0:T(8,128)}, u32[]{:S(2)}) copy-start(f32[512,384]{1,0:T(8,128)} %b_ref.1) | copy-start | bytes 2359300
  31.2 1.1 %copy-start.2 = (f32[160,8,128]{2,1,0:T(8,128)S(1)}, f32[160,8,128]{2,1,0:T(8,128)}, u32[]{:S(2)}) copy-start(f32[160,8,128]{2,1,0:T(8,128)} %get-tuple-element.11.p_ref) | copy-start | bytes 1966084
  32.2 1.0 %copy-start.3 = (f32[2,512,128]{2,1,0:T(8,128)S(1)}, f32[2,512,128]{2,1,0:T(8,128)}, u32[]{:S(2)}) copy-start(f32[2,512,128]{2,1,0:T(8,128)} %get-tuple-element.12.t_ref) | copy-start | bytes 1572868
  33.3 24.8 %copy-start = (f32[16,512,128]{2,1,0:T(8,128)S(1)}, f32[16,512,128]{2,1,0:T(8,128)}, u32[]{:S(2)}) copy-start(f32[16,512,128]{2,1,0:T(8,128)} %t_ref.3) | copy-start | bytes 12582916

commit v8 on v6

--- a/solution.py
+++ b/solution.py
@@ -12,7 +12,7 @@
 NT = (((1,), (1,)), ((), ()))
 
 
-def ar_kernel(t_ref, o_ref, tbuf, hb, lb, gp, ra, aa, rb, ab, rc, ac, tsem, sa, qa, sb, qb, sc, qc, sd, qd, se, qe):
+def ar_kernel(t_ref, o_ref, hb, lb, gp, ra, aa, rb, ab, rc, ac, sa, qa, sb, qb, sc, qc, sd, qd, se, qe):
     gx = lax.axis_index("gx")
     gy = lax.axis_index("gy")
     x, y, z, c = gx // 4, gx % 4, gy // 2, gy % 2
@@ -22,9 +22,6 @@
         dx, dy = OFFS[k]
         return ((x + sign * dx + 4) % 4) * 4 + (y + sign * dy + 4) % 4
 
-    loads = [pltpu.make_async_copy(t_ref.at[pl.ds(4 * i, 4)], tbuf.at[pl.ds(4 * i, 4)], tsem.at[i]) for i in range(4)]
-    for cp in loads:
-        cp.start()
     barrier = pltpu.get_barrier_semaphore()
     pl.semaphore_signal(barrier, inc=1, device_id=(gx, mate), device_id_type=MESH)
     for k in range(15):
@@ -32,30 +29,22 @@
     for d in range(1, 4):
         pl.semaphore_signal(barrier, inc=1, device_id=(gx, ((z + d) % 4) * 2 + c), device_id_type=MESH)
 
+    for s in range(16):
+        v = t_ref[s]
+        h = v.astype(BF)
+        hb[:, 128 * s:128 * s + 128] = h
+        lb[:, 128 * s:128 * s + 128] = (v - h.astype(jnp.float32)).astype(BF)
+
     def dot(a, b):
         return lax.dot_general(a, b, NT, preferred_element_type=jnp.float32)
 
-    for i in range(4):
-        loads[i].wait()
-        for s in range(4 * i, 4 * i + 4):
-            v = tbuf[s]
-            h = v.astype(BF)
-            hb[:, 128 * s:128 * s + 128] = h
-            lb[:, 128 * s:128 * s + 128] = (v - h.astype(jnp.float32)).astype(BF)
-        if i % 2 == 0:
-            continue
-        ks = slice(1024 * (i // 2), 1024 * (i // 2) + 1024)
-        for (r0, c0) in ((0, 0), (256, 0), (256, 256)):
-            hr, lr = hb[r0:r0 + 256, ks], lb[r0:r0 + 256, ks]
-            hc, lc = hb[c0:c0 + 256, ks], lb[c0:c0 + 256, ks]
-            g = dot(hr, hc) + dot(hr, lc) + dot(lr, hc)
-            for n, (bi, bj) in enumerate(BLOCKS):
-                if r0 <= 128 * bi < r0 + 256 and c0 <= 128 * bj < c0 + 256:
-                    part = g[128 * bi - r0:128 * bi - r0 + 128, 128 * bj - c0:128 * bj - c0 + 128].reshape(16, 8, 128)
-                    if i == 1:
-                        gp[16 * n:16 * n + 16] = part
-                    else:
-                        gp[16 * n:16 * n + 16] += part
+    for (r0, c0) in ((0, 0), (256, 0), (256, 256)):
+        hr, lr = hb[r0:r0 + 256, :], lb[r0:r0 + 256, :]
+        hc, lc = hb[c0:c0 + 256, :], lb[c0:c0 + 256, :]
+        g = dot(hr, hc) + dot(hr, lc) + dot(lr, hc)
+        for n, (i, j) in enumerate(BLOCKS):
+            if r0 <= 128 * i < r0 + 256 and c0 <= 128 * j < c0 + 256:
+                gp[16 * n:16 * n + 16] = g[128 * i - r0:128 * i - r0 + 128, 128 * j - c0:128 * j - c0 + 128].reshape(16, 8, 128)
 
     pl.semaphore_wait(barrier, 19)
     pieces = lambda core, g: pl.ds(80 * core + 5 * g, 5)
@@ -116,15 +105,15 @@
     return pl.pallas_call(
         ar_kernel,
         out_shape=jax.ShapeDtypeStruct((160, 8, 128), f),
-        in_specs=[pl.BlockSpec(memory_space=pl.ANY)],
+        in_specs=[pl.BlockSpec(memory_space=pltpu.VMEM)],
         out_specs=pl.BlockSpec(memory_space=pltpu.VMEM),
         scratch_shapes=[
-            V((16, 512, 128), f), V((512, 2048), BF), V((512, 2048), BF),
+            V((512, 2048), BF), V((512, 2048), BF),
             V((160, 8, 128), f), V((16, 5, 8, 128), f), V((16, 5, 8, 128), f), V((16, 5, 8, 128), f),
             V((5, 8, 128), f), V((4, 5, 8, 128), f), V((5, 8, 128), f),
-            D((4,)), D((16,)), D((16,)), D((16,)), D((16,)), D((4,)), D((4,)), D((16,)), D((16,)), D((16,)), D((16,)),
+            D((16,)), D((16,)), D((16,)), D((16,)), D((4,)), D((4,)), D((16,)), D((16,)), D((16,)), D((16,)),
         ],
-        compiler_params=pltpu.CompilerParams(collective_id=0, has_side_effects=True, vmem_limit_bytes=60 << 20),
+        compiler_params=pltpu.CompilerParams(collective_id=0, has_side_effects=True, vmem_limit_bytes=28 << 20),
         name="gram_sum",
     )(tensor)
 
@@ -310,7 +299,7 @@
 GROUPS = [(0, 2), (2, 4), (4, 8), (8, 12), (12, 16)]
 
 
-def core_kernel(q_ref, t_ref, o_ref, tbuf, qh, ql, y, tsem, ssem, rsem, osem):
+def core_kernel(q_ref, t_ref, o_ref, qh, ql, y, ssem, rsem, osem):
     gx = lax.axis_index("gx")
     gy = lax.axis_index("gy")
     z, c = gy // 2, gy % 2
@@ -319,9 +308,6 @@
         dz, dc = RELS[r]
         return ((z + dz) % 4) * 2 + (c + dc) % 2
 
-    loads = [pltpu.make_async_copy(t_ref.at[pl.ds(a, b - a)], tbuf.at[pl.ds(a, b - a)], tsem.at[n]) for n, (a, b) in enumerate(GROUPS)]
-    for cp in loads:
-        cp.start()
     barrier = pltpu.get_barrier_semaphore()
     for r in range(7):
         pl.semaphore_signal(barrier, inc=1, device_id=(gx, other(r)), device_id_type=pl.DeviceIdType.MESH)
@@ -336,9 +322,8 @@
     spot = pl.ds(pl.multiple_of(gy * 128, 128), 128)
     sends = []
     for n, (a, b) in enumerate(GROUPS):
-        loads[n].wait()
         for k in range(a, b, 2):
-            v = jnp.concatenate([tbuf[k], tbuf[k + 1]], axis=1)
+            v = jnp.concatenate([t_ref[k], t_ref[k + 1]], axis=1)
             th = v.astype(jnp.bfloat16)
             tl = (v - th.astype(jnp.float32)).astype(jnp.bfloat16)
             out = dot(qh[...], th) + dot(qh[...], tl) + dot(ql[...], th)
@@ -368,11 +353,11 @@
     return pl.pallas_call(
         core_kernel,
         out_shape=jax.ShapeDtypeStruct((16, 48, 1024), f),
-        in_specs=[pl.BlockSpec(memory_space=pltpu.VMEM), pl.BlockSpec(memory_space=pl.ANY)],
+        in_specs=[pl.BlockSpec(memory_space=pltpu.VMEM), pl.BlockSpec(memory_space=pltpu.VMEM)],
         out_specs=pl.BlockSpec(memory_space=pltpu.VMEM),
-        scratch_shapes=[V((16, 512, 128), f), V((384, 512), jnp.bfloat16), V((384, 512), jnp.bfloat16), V((16, 384, 128), f),
-                        D((ng,)), D((7, ng)), D((7, ng)), D],
-        compiler_params=pltpu.CompilerParams(collective_id=1, has_side_effects=True, vmem_limit_bytes=24 << 20),
+        scratch_shapes=[V((384, 512), jnp.bfloat16), V((384, 512), jnp.bfloat16), V((16, 384, 128), f),
+                        D((7, ng)), D((7, ng)), D],
+        compiler_params=pltpu.CompilerParams(collective_id=1, has_side_effects=True, vmem_limit_bytes=20 << 20),
         name="core_out",
     )(basis_t, tensor)
 

time: 92.3 us -> 89.3 us (0.967)
  Pallas kernels: 89.4 us -> 85.3 us
  local copies, waits for them, and re-layouts: 2.75 us -> 3.86 us
    pallas_call x1, Pallas kernels: 31.9 us -> 28.4 us  [gram_sum(): pl.pallas_call(ar_kernel, out_shape=jax.ShapeDtypeStruct((160, 8, 128), f...]
    unnamed x7 -> x5, local copies, waits for them, and re-layouts: 2.75 us -> 3.86 us
where the time goes in v8:
time: 89.3 us; the launch traced here: 89.2 us
  Pallas kernels  85.3 us (96%)
  local copies, waits for them, and re-layouts  3.86 us (4%)
    pallas_call x1, Pallas kernels, core_out(): pl.pallas_call(core_kernel, out_shape=jax.ShapeDtypeStruct((16, 48, 1024)...  38.1 us
    pallas_call x1, Pallas kernels, gram_sum(): pl.pallas_call(ar_kernel, out_shape=jax.ShapeDtypeStruct((160, 8, 128), f...  28.4 us
    pallas_call x1, Pallas kernels, sweeps(): pl.pallas_call(sweeps_kernel, out_shape=jax.ShapeDtypeStruct((384, 512),...  18.8 us
    unnamed x5, local copies, waits for them, and re-layouts  3.86 us

profile of v8, /device:TPU:1, one launch (start us, length us, event | category | flops | bytes accessed | tf_op | source)
XLA Modules:
  0.0 89.2 jit_solution(5071494259723135264)
XLA Ops:
  0.0 0.0 copy-start
  0.0 2.2 %copy-done = f32[16,512,128]{2,1,0:T(8,128)S(1)} copy-done((f32[16,512,128]{2,1,0:T(8,128)S(1)}, f32[16,512,128]{2,1,0:T(8,128)}, u32[]{:S(2)}) %copy-start) | copy-done | bytes 4194328
  2.2 0.0 copy-start.1
  2.2 28.4 %gram_sum.1.p_ref = f32[160,8,128]{2,1,0:T(8,128)S(1)} custom-call(f32[16,512,128]{2,1,0:T(8,128)S(1)} %copy-done), custom_call_target="tpu_custom_call" | custom-call | tf_op jit(solution)/shard_map/gram_sum/pallas_call | solution.py:105
  30.6 0.0 copy-done.1
  30.6 18.8 %sweeps.1.q_ref = f32[384,512]{1,0:T(8,128)S(1)} custom-call(f32[160,8,128]{2,1,0:T(8,128)S(1)} %gram_sum.1.p_ref, f32[512,384]{1,0:T(8,128)S(1)} %copy-done.1), custom_call_target="tpu_custom_call" | custom-call | flops 4000000000 | bytes 3000000 | tf_op jit(solution)/shard_map/sweeps/pallas_call | solution.py:287
  49.4 38.1 %core_out.1 = f32[16,48,1024]{2,1,0:T(8,128)S(1)} custom-call(f32[384,512]{1,0:T(8,128)S(1)} %sweeps.1.q_ref, f32[16,512,128]{2,1,0:T(8,128)S(1)} %copy-done), custom_call_target="tpu_custom_call" | custom-call | tf_op jit(solution)/shard_map/core_out/pallas_call | solution.py:353
  87.5 1.7 %copy.4 = f32[16,48,1024]{2,1,0:T(8,128)} copy(f32[16,48,1024]{2,1,0:T(8,128)S(1)} %core_out.1) | data formatting | bytes 6291456
Async XLA Ops:
  0.0 2.2 %copy-start = (f32[16,512,128]{2,1,0:T(8,128)S(1)}, f32[16,512,128]{2,1,0:T(8,128)}, u32[]{:S(2)}) copy-start(f32[16,512,128]{2,1,0:T(8,128)} %t_ref.3) | copy-start | bytes 12582916
  2.2 28.4 %copy-start.1 = (f32[512,384]{1,0:T(8,128)S(1)}, f32[512,384]{1,0:T(8,128)}, u32[]{:S(2)}) copy-start(f32[512,384]{1,0:T(8,128)} %b_ref.1) | copy-start | bytes 2359300

commit v9 on v8

--- a/solution.py
+++ b/solution.py
@@ -113,9 +113,12 @@
             V((5, 8, 128), f), V((4, 5, 8, 128), f), V((5, 8, 128), f),
             D((16,)), D((16,)), D((16,)), D((16,)), D((4,)), D((4,)), D((16,)), D((16,)), D((16,)), D((16,)),
         ],
-        compiler_params=pltpu.CompilerParams(collective_id=0, has_side_effects=True, vmem_limit_bytes=28 << 20),
+        compiler_params=pltpu.CompilerParams(collective_id=0, has_side_effects=True, vmem_limit_bytes=16 << 20),
         name="gram_sum",
     )(tensor)
+
+
+KG = 2
 
 
 def split(x):
@@ -210,7 +213,21 @@
                 steps.remove(one)
 
 
-def sweeps_kernel(p_ref, b_ref, o_ref, g_ref, p, q, a, li, one_ref):
+def sweeps_kernel(p_ref, b_ref, t_ref, o_ref, below, above, g_ref, p, q, a, li, one_ref, ssem, rsem):
+    gx = lax.axis_index("gx")
+    gy = lax.axis_index("gy")
+    up, down = (gy + 2) % 8, (gy + 6) % 8
+    barrier = pltpu.get_barrier_semaphore()
+    for dev in (up, down):
+        pl.semaphore_signal(barrier, inc=1, device_id=(gx, dev), device_id_type=pl.DeviceIdType.MESH)
+    moves = []
+
+    def move(src, dst, dev):
+        n = len(moves)
+        cp = pltpu.make_async_remote_copy(src_ref=src, dst_ref=dst, send_sem=ssem.at[n], recv_sem=rsem.at[n], device_id=(gx, dev), device_id_type=pl.DeviceIdType.MESH)
+        cp.start()
+        moves.append(cp)
+
     n = 0
     for i in range(4):
         for j in range(i + 1):
@@ -219,6 +236,10 @@
             if j < i:
                 g_ref[128 * j:128 * j + 128, 128 * i:128 * i + 128] = blk.T
             n += 1
+    pl.semaphore_wait(barrier, 2)
+    for n in range(KG):
+        move(t_ref.at[n], below.at[n], up)
+        move(t_ref.at[n], above.at[n], down)
     one_ref[...] = jnp.ones((8, 128), jnp.float32)
     one = one_ref[...]
     first, second = 0, 3
@@ -279,27 +300,31 @@
     basis(second, 2)
     for k in range(3):
         o_ref[128 * k:128 * k + 128, :] = q[3 + k]
-
-
-def sweeps(packed, start):
+    for cp in moves:
+        cp.wait()
+
+
+def sweeps(packed, start, tensor):
     f = jnp.float32
     whole = pl.BlockSpec(memory_space=pltpu.VMEM)
+    anywhere = pl.BlockSpec(memory_space=pl.ANY)
     return pl.pallas_call(
         sweeps_kernel,
-        out_shape=jax.ShapeDtypeStruct((384, 512), f),
-        in_specs=[whole] * 2, out_specs=whole,
+        out_shape=(jax.ShapeDtypeStruct((384, 512), f),) + (jax.ShapeDtypeStruct((KG, 512, 128), f),) * 2,
+        in_specs=[whole] * 2 + [anywhere], out_specs=(whole,) + (anywhere,) * 2,
         scratch_shapes=[pltpu.VMEM((512, 512), f), pltpu.VMEM((6, 128, 512), f), pltpu.VMEM((6, 128, 512), f),
-                        pltpu.VMEM((6, 3, 128, 128), f), pltpu.VMEM((6, 128, 128), f), pltpu.VMEM((8, 128), f)],
+                        pltpu.VMEM((6, 3, 128, 128), f), pltpu.VMEM((6, 128, 128), f), pltpu.VMEM((8, 128), f),
+                        pltpu.SemaphoreType.DMA((2 * KG,)), pltpu.SemaphoreType.DMA((2 * KG,))],
         cost_estimate=pl.CostEstimate(flops=4000000000, bytes_accessed=3000000, transcendentals=0),
-        compiler_params=pltpu.CompilerParams(vmem_limit_bytes=24 << 20), name="sweeps",
-    )(packed, start)
+        compiler_params=pltpu.CompilerParams(collective_id=2, has_side_effects=True, vmem_limit_bytes=12 << 20), name="sweeps",
+    )(packed, start, tensor)
 
 
 RELS = [(2, 0), (2, 1), (1, 0), (3, 0), (1, 1), (3, 1), (0, 1)]
-GROUPS = [(0, 2), (2, 4), (4, 8), (8, 12), (12, 16)]
-
-
-def core_kernel(q_ref, t_ref, o_ref, qh, ql, y, ssem, rsem, osem):
+GROUPS = [(2, 4), (4, 6), (6, 10), (10, 16), (0, KG)]
+
+
+def core_kernel(q_ref, t_ref, below, above, o_ref, qh, ql, y, yg, ssem, rsem, xsem, wsem, osem):
     gx = lax.axis_index("gx")
     gy = lax.axis_index("gy")
     z, c = gy // 2, gy % 2
@@ -332,6 +357,8 @@
         if n == 0:
             pl.semaphore_wait(barrier, 7)
         for r in range(7):
+            if b <= KG and RELS[r][0] % 2 == 1:
+                continue
             cp = pltpu.make_async_remote_copy(
                 src_ref=y.at[pl.ds(a, b - a), pl.ds(pl.multiple_of(48 * other(r), 8), 48)],
                 dst_ref=o_ref.at[pl.ds(a, b - a), pl.ds(0, 48), spot],
@@ -339,31 +366,57 @@
                 device_id=(gx, other(r)), device_id_type=pl.DeviceIdType.MESH)
             cp.start()
             sends.append(cp)
-    own = pltpu.make_async_copy(y.at[pl.ds(0, 16), pl.ds(pl.multiple_of(48 * gy, 8), 48)], o_ref.at[pl.ds(0, 16), pl.ds(0, 48), spot], osem)
+    own = pltpu.make_async_copy(y.at[pl.ds(0, 16), pl.ds(pl.multiple_of(48 * gy, 8), 48)], o_ref.at[pl.ds(0, 16), pl.ds(0, 48), spot], osem.at[2])
     own.start()
+    rows = pl.ds(pl.multiple_of(96 * z, 32), 96)
+    q2 = jnp.concatenate([qh[rows, :], ql[rows, :]], axis=0)
+    locs = [own]
+    for s, (got, dz) in enumerate(((below, 3), (above, 1))):
+        for k in range(0, KG, 2):
+            v = jnp.concatenate([got[k], got[k + 1]], axis=1)
+            th = v.astype(jnp.bfloat16)
+            tl = (v - th.astype(jnp.float32)).astype(jnp.bfloat16)
+            o2 = dot(q2, th)
+            out = o2[:96] + o2[96:] + dot(q2[:96], tl)
+            for d in range(2):
+                yg[s, 0, k + d] = out[:48, 128 * d:128 * d + 128]
+                yg[s, 1, k + d] = out[48:, 128 * d:128 * d + 128]
+        src = ((z + dz) % 4) * 2 + c
+        there = pl.ds(pl.multiple_of(src * 128, 128), 128)
+        cp = pltpu.make_async_remote_copy(
+            src_ref=yg.at[s, 1 - c], dst_ref=o_ref.at[pl.ds(0, KG), pl.ds(0, 48), there],
+            send_sem=xsem.at[s], recv_sem=wsem.at[s],
+            device_id=(gx, z * 2 + 1 - c), device_id_type=pl.DeviceIdType.MESH)
+        cp.start()
+        sends.append(cp)
+        cp = pltpu.make_async_copy(yg.at[s, c], o_ref.at[pl.ds(0, KG), pl.ds(0, 48), there], osem.at[s])
+        cp.start()
+        locs.append(cp)
     for cp in sends:
         cp.wait()
-    own.wait()
-
-
-def core_out(basis_t, tensor):
+    for cp in locs:
+        cp.wait()
+
+
+def core_out(basis_t, tensor, below, above):
     f = jnp.float32
     V, D = pltpu.VMEM, pltpu.SemaphoreType.DMA
     ng = len(GROUPS)
     return pl.pallas_call(
         core_kernel,
         out_shape=jax.ShapeDtypeStruct((16, 48, 1024), f),
-        in_specs=[pl.BlockSpec(memory_space=pltpu.VMEM), pl.BlockSpec(memory_space=pltpu.VMEM)],
+        in_specs=[pl.BlockSpec(memory_space=pltpu.VMEM)] * 4,
         out_specs=pl.BlockSpec(memory_space=pltpu.VMEM),
-        scratch_shapes=[V((384, 512), jnp.bfloat16), V((384, 512), jnp.bfloat16), V((16, 384, 128), f),
-                        D((7, ng)), D((7, ng)), D],
+        scratch_shapes=[V((384, 512), jnp.bfloat16), V((384, 512), jnp.bfloat16), V((16, 384, 128), f), V((2, 2, KG, 48, 128), f),
+                        D((7, ng)), D((7, ng)), D((2,)), D((2,)), D((3,))],
         compiler_params=pltpu.CompilerParams(collective_id=1, has_side_effects=True, vmem_limit_bytes=20 << 20),
         name="core_out",
-    )(basis_t, tensor)
+    )(basis_t, tensor, below, above)
 
 
 def body(tensor, start_basis):
-    return core_out(sweeps(gram_sum(tensor), start_basis), tensor)
+    basis_t, below, above = sweeps(gram_sum(tensor), start_basis, tensor)
+    return core_out(basis_t, tensor, below, above)
 
 
 def solution(mesh):

time: 89.3 us -> 90.1 us (level)
  local copies, waits for them, and re-layouts: 3.86 us -> 4.99 us
    unnamed x5 -> x7, local copies, waits for them, and re-layouts: 3.86 us -> 4.99 us
where the time goes in v9:
time: 90.1 us; the launch traced here: 89.9 us
  Pallas kernels  84.9 us (94%)
  local copies, waits for them, and re-layouts  4.99 us (6%)
    pallas_call x1, Pallas kernels, core_out(): pl.pallas_call(core_kernel, out_shape=jax.ShapeDtypeStruct((16, 48, 1024)...  37.5 us
    pallas_call x1, Pallas kernels, gram_sum(): pl.pallas_call(ar_kernel, out_shape=jax.ShapeDtypeStruct((160, 8, 128), f...  28.4 us
    pallas_call x1, Pallas kernels, sweeps(): pl.pallas_call(sweeps_kernel, out_shape=(jax.ShapeDtypeStruct((384, 512),...  19 us
    unnamed x7, local copies, waits for them, and re-layouts  4.99 us

profile of v9, /device:TPU:1, one launch (start us, length us, event | category | flops | bytes accessed | tf_op | source)
XLA Modules:
  0.0 89.9 jit_solution(8595148745793300801)
XLA Ops:
  0.0 0.0 copy-start
  0.0 2.2 %copy-done = f32[16,512,128]{2,1,0:T(8,128)S(1)} copy-done((f32[16,512,128]{2,1,0:T(8,128)S(1)}, f32[16,512,128]{2,1,0:T(8,128)}, u32[]{:S(2)}) %copy-start) | copy-done | bytes 4194328
  2.2 0.0 copy-start.1
  2.2 28.4 %gram_sum.1.p_ref = f32[160,8,128]{2,1,0:T(8,128)S(1)} custom-call(f32[16,512,128]{2,1,0:T(8,128)S(1)} %copy-done), custom_call_target="tpu_custom_call" | custom-call | tf_op jit(solution)/shard_map/gram_sum/pallas_call | solution.py:105
  30.6 0.0 copy-done.1
  30.6 0.0 copy-start.2
  30.6 1.1 %copy-done.2 = f32[512,384]{1,0:T(8,128)S(1)} copy-done((f32[512,384]{1,0:T(8,128)S(1)}, f32[512,384]{1,0:T(8,128)}, u32[]{:S(2)}) %copy-start.2) | copy-done | bytes 786456
  31.7 19.0 %sweeps.1 = (f32[384,512]{1,0:T(8,128)S(1)}, f32[2,512,128]{2,1,0:T(8,128)S(1)}, f32[2,512,128]{2,1,0:T(8,128)S(1)}) custom-call(f32[160,8,128]{2,1,0:T(8,128)S(1)} %gram_sum.1.p_ref, f32[512,384]{1,0:T(8,128)S(1)} %copy-done.2, f32[16,512,128]{2,1,0:T(8,128)S(1)} %copy-done.1), custom_call_target="tpu_custom_call" | custom-call | flops 4000000000 | bytes 3000000 | tf_op jit(solution)/shard_map/sweeps/pallas_call | solution.py:311
  50.8 37.5 %core_out.1 = f32[16,48,1024]{2,1,0:T(8,128)S(1)} custom-call(f32[384,512]{1,0:T(8,128)S(1)} %get-tuple-element.8.q_ref, f32[16,512,128]{2,1,0:T(8,128)S(1)} %copy-done.1, f32[2,512,128]{2,1,0:T(8,128)S(1)} %get-tuple-element.9.below, f32[2,512,128]{2,1,0:T(8,128)S(1)} %get-tuple-element.10.above), custom_call_target="tpu_custom_call" | custom-call | tf_op jit(solution)/shard_map/core_out/pallas_call | solution.py:405
  88.3 1.7 %copy.4 = f32[16,48,1024]{2,1,0:T(8,128)} copy(f32[16,48,1024]{2,1,0:T(8,128)S(1)} %core_out.1) | data formatting | bytes 6291456
Async XLA Ops:
  0.0 2.2 %copy-start = (f32[16,512,128]{2,1,0:T(8,128)S(1)}, f32[16,512,128]{2,1,0:T(8,128)}, u32[]{:S(2)}) copy-start(f32[16,512,128]{2,1,0:T(8,128)} %t_ref.5) | copy-start | bytes 12582916
  2.2 28.4 %copy-start.1 = (f32[16,512,128]{2,1,0:T(8,128)S(1)}, f32[16,512,128]{2,1,0:T(8,128)}, u32[]{:S(2)}) copy-start(f32[16,512,128]{2,1,0:T(8,128)} %t_ref.5) | copy-start | bytes 12582916
  30.6 1.1 %copy-start.2 = (f32[512,384]{1,0:T(8,128)S(1)}, f32[512,384]{1,0:T(8,128)}, u32[]{:S(2)}) copy-start(f32[512,384]{1,0:T(8,128)} %b_ref.1) | copy-start | bytes 2359300

commit v10 on v8

--- a/solution.py
+++ b/solution.py
@@ -296,7 +296,7 @@
 
 
 RELS = [(2, 0), (2, 1), (1, 0), (3, 0), (1, 1), (3, 1), (0, 1)]
-GROUPS = [(0, 2), (2, 4), (4, 8), (8, 12), (12, 16)]
+GROUPS = [(0, 2), (2, 6), (6, 16)]
 
 
 def core_kernel(q_ref, t_ref, o_ref, qh, ql, y, ssem, rsem, osem):

time: 89.3 us -> 89.1 us (level)
  no operation moved by 1% of the time
where the time goes in v10:
time: 89.1 us; the launch traced here: 89 us
  Pallas kernels  85.1 us (96%)
  local copies, waits for them, and re-layouts  3.86 us (4%)
    pallas_call x1, Pallas kernels, core_out(): pl.pallas_call(core_kernel, out_shape=jax.ShapeDtypeStruct((16, 48, 1024)...  37.9 us
    pallas_call x1, Pallas kernels, gram_sum(): pl.pallas_call(ar_kernel, out_shape=jax.ShapeDtypeStruct((160, 8, 128), f...  28.4 us
    pallas_call x1, Pallas kernels, sweeps(): pl.pallas_call(sweeps_kernel, out_shape=jax.ShapeDtypeStruct((384, 512),...  18.8 us
    unnamed x5, local copies, waits for them, and re-layouts  3.86 us

profile of v10, /device:TPU:1, one launch (start us, length us, event | category | flops | bytes accessed | tf_op | source)
XLA Modules:
  0.0 89.0 jit_solution(11686680195645357897)
XLA Ops:
  0.0 0.0 copy-start
  0.0 2.2 %copy-done = f32[16,512,128]{2,1,0:T(8,128)S(1)} copy-done((f32[16,512,128]{2,1,0:T(8,128)S(1)}, f32[16,512,128]{2,1,0:T(8,128)}, u32[]{:S(2)}) %copy-start) | copy-done | bytes 4194328
  2.2 0.0 copy-start.1
  2.2 28.4 %gram_sum.1.p_ref = f32[160,8,128]{2,1,0:T(8,128)S(1)} custom-call(f32[16,512,128]{2,1,0:T(8,128)S(1)} %copy-done), custom_call_target="tpu_custom_call" | custom-call | tf_op jit(solution)/shard_map/gram_sum/pallas_call | solution.py:105
  30.6 0.0 copy-done.1
  30.6 18.8 %sweeps.1.q_ref = f32[384,512]{1,0:T(8,128)S(1)} custom-call(f32[160,8,128]{2,1,0:T(8,128)S(1)} %gram_sum.1.p_ref, f32[512,384]{1,0:T(8,128)S(1)} %copy-done.1), custom_call_target="tpu_custom_call" | custom-call | flops 4000000000 | bytes 3000000 | tf_op jit(solution)/shard_map/sweeps/pallas_call | solution.py:287
  49.4 37.9 %core_out.1 = f32[16,48,1024]{2,1,0:T(8,128)S(1)} custom-call(f32[384,512]{1,0:T(8,128)S(1)} %sweeps.1.q_ref, f32[16,512,128]{2,1,0:T(8,128)S(1)} %copy-done), custom_call_target="tpu_custom_call" | custom-call | tf_op jit(solution)/shard_map/core_out/pallas_call | solution.py:353
  87.3 1.7 %copy.4 = f32[16,48,1024]{2,1,0:T(8,128)} copy(f32[16,48,1024]{2,1,0:T(8,128)S(1)} %core_out.1) | data formatting | bytes 6291456
Async XLA Ops:
  0.0 2.2 %copy-start = (f32[16,512,128]{2,1,0:T(8,128)S(1)}, f32[16,512,128]{2,1,0:T(8,128)}, u32[]{:S(2)}) copy-start(f32[16,512,128]{2,1,0:T(8,128)} %t_ref.3) | copy-start | bytes 12582916
  2.2 28.4 %copy-start.1 = (f32[512,384]{1,0:T(8,128)S(1)}, f32[512,384]{1,0:T(8,128)}, u32[]{:S(2)}) copy-start(f32[512,384]{1,0:T(8,128)} %b_ref.1) | copy-start | bytes 2359300

commit v11 on v10

--- a/solution.py
+++ b/solution.py
@@ -296,7 +296,7 @@
 
 
 RELS = [(2, 0), (2, 1), (1, 0), (3, 0), (1, 1), (3, 1), (0, 1)]
-GROUPS = [(0, 2), (2, 6), (6, 16)]
+GROUPS = [(0, 4), (4, 16)]
 
 
 def core_kernel(q_ref, t_ref, o_ref, qh, ql, y, ssem, rsem, osem):

time: 89.1 us -> 89 us (level)
  no operation moved by 1% of the time
where the time goes in v11:
time: 89 us; the launch traced here: 88.8 us
  Pallas kernels  84.9 us (95%)
  local copies, waits for them, and re-layouts  3.86 us (4%)
    pallas_call x1, Pallas kernels, core_out(): pl.pallas_call(core_kernel, out_shape=jax.ShapeDtypeStruct((16, 48, 1024)...  37.7 us
    pallas_call x1, Pallas kernels, gram_sum(): pl.pallas_call(ar_kernel, out_shape=jax.ShapeDtypeStruct((160, 8, 128), f...  28.4 us
    pallas_call x1, Pallas kernels, sweeps(): pl.pallas_call(sweeps_kernel, out_shape=jax.ShapeDtypeStruct((384, 512),...  18.8 us
    unnamed x5, local copies, waits for them, and re-layouts  3.86 us

profile of v11, /device:TPU:1, one launch (start us, length us, event | category | flops | bytes accessed | tf_op | source)
XLA Modules:
  0.0 88.8 jit_solution(7274711227197559465)
XLA Ops:
  0.0 0.0 copy-start
  0.0 2.2 %copy-done = f32[16,512,128]{2,1,0:T(8,128)S(1)} copy-done((f32[16,512,128]{2,1,0:T(8,128)S(1)}, f32[16,512,128]{2,1,0:T(8,128)}, u32[]{:S(2)}) %copy-start) | copy-done | bytes 4194328
  2.2 0.0 copy-start.1
  2.2 28.4 %gram_sum.1.p_ref = f32[160,8,128]{2,1,0:T(8,128)S(1)} custom-call(f32[16,512,128]{2,1,0:T(8,128)S(1)} %copy-done), custom_call_target="tpu_custom_call" | custom-call | tf_op jit(solution)/shard_map/gram_sum/pallas_call | solution.py:105
  30.6 0.0 copy-done.1
  30.6 18.8 %sweeps.1.q_ref = f32[384,512]{1,0:T(8,128)S(1)} custom-call(f32[160,8,128]{2,1,0:T(8,128)S(1)} %gram_sum.1.p_ref, f32[512,384]{1,0:T(8,128)S(1)} %copy-done.1), custom_call_target="tpu_custom_call" | custom-call | flops 4000000000 | bytes 3000000 | tf_op jit(solution)/shard_map/sweeps/pallas_call | solution.py:287
  49.4 37.7 %core_out.1 = f32[16,48,1024]{2,1,0:T(8,128)S(1)} custom-call(f32[384,512]{1,0:T(8,128)S(1)} %sweeps.1.q_ref, f32[16,512,128]{2,1,0:T(8,128)S(1)} %copy-done), custom_call_target="tpu_custom_call" | custom-call | tf_op jit(solution)/shard_map/core_out/pallas_call | solution.py:353
  87.2 1.7 %copy.4 = f32[16,48,1024]{2,1,0:T(8,128)} copy(f32[16,48,1024]{2,1,0:T(8,128)S(1)} %core_out.1) | data formatting | bytes 6291456
Async XLA Ops:
  0.0 2.2 %copy-start = (f32[16,512,128]{2,1,0:T(8,128)S(1)}, f32[16,512,128]{2,1,0:T(8,128)}, u32[]{:S(2)}) copy-start(f32[16,512,128]{2,1,0:T(8,128)} %t_ref.3) | copy-start | bytes 12582916
  2.2 28.4 %copy-start.1 = (f32[512,384]{1,0:T(8,128)S(1)}, f32[512,384]{1,0:T(8,128)}, u32[]{:S(2)}) copy-start(f32[512,384]{1,0:T(8,128)} %b_ref.1) | copy-start | bytes 2359300
